TPU v7x, 256 devices: a whole 4x4x8 slice. The times are simulated.
256 devices in a mesh: seq: 64 (over y, z, core), head: 4 (over x).
Axes of the slice: x: 4, y: 4, z: 8, core: 2. Of those that a mesh axis runs over, the one named last changes fastest.
Arguments:
- queries: bfloat16 [65536, 1024], P('seq', 'head'), may hold values from -6 to 6
- keys: bfloat16 [65536, 1024], P('seq', 'head'), may hold values from -12 to 12
- values: bfloat16 [65536, 1024], P('seq', 'head'), may hold values from -6 to 6
- out_weight: bfloat16 [1024, 1024], P('head'), may hold values from -0.1875 to 0.1875
- cotangent: bfloat16 [65536, 1024], P('seq', 'head'), may hold values from -6 to 6
Outputs:
- output: bfloat16 [65536, 1024], P('seq', 'head')
- query_grad: bfloat16 [65536, 1024], P('seq', 'head')
- key_grad: bfloat16 [65536, 1024], P('seq', 'head')
- value_grad: bfloat16 [65536, 1024], P('seq', 'head')
- weight_grad: float32 [1024, 1024], P('head')
All inputs are finite; a program needn't handle non-finite values.
Results may differ from a plain program's by a relative error of at most 0.015.
Values may be sent and summed in bfloat16 or wider, within the bound.
A program may use at most 128 MiB of HBM per device.

v0:
```python
import jax
import jax.numpy as jnp
from jax import lax
from jax.sharding import PartitionSpec as P

TILE = 128
DH = 128


def from_behind(x, axis, by):
    size = lax.axis_size(axis)
    pairs = [(i, i + by) for i in range(size) if 0 <= i + by < size]
    return lax.ppermute(x, axis, pairs)


def local(queries, keys, values, out_weight, cotangent):
    rows, width = queries.shape
    heads = width // DH
    seq_count = lax.axis_size("seq")
    levels = seq_count.bit_length() - 1
    my_block = lax.axis_index("seq")
    scale = DH ** (-0.5)
    tile_pair = (keys[rows - TILE :], values[rows - TILE :])
    key_tiles = []
    value_tiles = []
    for level_idx in range(levels):
        got_keys, got_values = from_behind((tile_pair[0], tile_pair[1]), "seq", 2**level_idx)
        key_tiles.append(got_keys)
        value_tiles.append(got_values)
    offsets = (2 ** jnp.arange(levels)).astype(jnp.int32)
    tile_valid = jnp.repeat(my_block - offsets >= 0, TILE)
    causal = jnp.arange(rows)[:, None] >= jnp.arange(rows)[None, :]
    allowed = jnp.concatenate(
        [causal, jnp.broadcast_to(tile_valid[None, :], (rows, levels * TILE))], axis=1
    )
    all_keys = jnp.concatenate([keys] + key_tiles, axis=0).reshape(-1, heads, DH)
    all_values = jnp.concatenate([values] + value_tiles, axis=0).reshape(-1, heads, DH)
    query_three = queries.reshape(rows, heads, DH)
    scores = (
        jnp.einsum("qhd,khd->hqk", query_three, all_keys, preferred_element_type=jnp.float32)
        * scale
    )
    scores = jnp.where(allowed[None], scores, -jnp.inf)
    top = jnp.max(scores, axis=-1, keepdims=True)
    expo = jnp.exp(scores - top)
    prob = expo / jnp.sum(expo, axis=-1, keepdims=True)
    prob_low = prob.astype(jnp.bfloat16)
    attn = jnp.einsum("hqk,khd->qhd", prob_low, all_values, preferred_element_type=jnp.float32)
    attn_flat = attn.astype(jnp.bfloat16).reshape(rows, width)
    partial_out = jnp.dot(attn_flat, out_weight, preferred_element_type=jnp.float32)
    output = lax.psum_scatter(
        partial_out.astype(jnp.bfloat16), "head", scatter_dimension=1, tiled=True
    )
    segment = lax.all_gather(cotangent, "head", axis=1, tiled=True)
    grad_attn = lax.dot_general(
        segment, out_weight, (((1,), (1,)), ((), ())), preferred_element_type=jnp.float32
    )
    block_terms = lax.dot_general(
        attn_flat, segment, (((0,), (0,)), ((), ())), preferred_element_type=jnp.float32
    )
    grad_weight = block_terms
    grad_attn, grad_weight = (grad_attn, grad_weight)
    weight_grad = lax.psum(grad_weight, "seq")
    dattn_three = grad_attn.astype(jnp.bfloat16).reshape(rows, heads, DH)
    dprob = jnp.einsum("qhd,khd->hqk", dattn_three, all_values, preferred_element_type=jnp.float32)
    value_terms = jnp.einsum(
        "hqk,qhd->khd", prob_low, dattn_three, preferred_element_type=jnp.float32
    )
    delta = jnp.sum(prob * dprob, axis=-1, keepdims=True)
    dscore = (prob * (dprob - delta)).astype(jnp.bfloat16)
    query_terms = (
        jnp.einsum("hqk,khd->qhd", dscore, all_keys, preferred_element_type=jnp.float32) * scale
    )
    key_terms = (
        jnp.einsum("hqk,qhd->khd", dscore, query_three, preferred_element_type=jnp.float32) * scale
    )
    key_flat = key_terms.reshape(-1, width)
    value_flat = value_terms.reshape(-1, width)
    key_tail = key_flat[rows - TILE : rows]
    value_tail = value_flat[rows - TILE : rows]
    for level_idx in range(levels):
        lower = rows + level_idx * TILE
        back_keys, back_values = (
            from_behind(
                key_flat[lower : lower + TILE].astype(jnp.bfloat16), "seq", -(2**level_idx)
            ).astype(jnp.float32),
            from_behind(
                value_flat[lower : lower + TILE].astype(jnp.bfloat16), "seq", -(2**level_idx)
            ).astype(jnp.float32),
        )
        key_tail = key_tail + back_keys
        value_tail = value_tail + back_values
    key_grad = jnp.concatenate([key_flat[: rows - TILE], key_tail], axis=0).astype(jnp.bfloat16)
    value_grad = jnp.concatenate([value_flat[: rows - TILE], value_tail], axis=0).astype(
        jnp.bfloat16
    )
    query_grad = query_terms.reshape(rows, width).astype(jnp.bfloat16)
    return (output, query_grad, key_grad, value_grad, weight_grad)


def solution(mesh):
    placed = (
        P("seq", "head"),
        P("seq", "head"),
        P("seq", "head"),
        P("head", None),
        P("seq", "head"),
    )
    return jax.shard_map(
        local,
        mesh=mesh,
        in_specs=placed,
        out_specs=(
            P("seq", "head"),
            P("seq", "head"),
            P("seq", "head"),
            P("seq", "head"),
            P("head", None),
        ),
        check_vma=False,
    )
```

profile of v0, /device:TPU:1, one launch (start us, length us, event | category | flops | bytes accessed | tf_op | source)
XLA Modules:
  0.0 330.4 jit_solution(2480007653751314)
XLA Ops:
  8.8 6.3 %collective-permute-start.5 = (bf16[128,256]{1,0:T(8,128)(2,1)}, bf16[128,256]{1,0:T(8,128)(2,1)}, u32[]{:S(2)}, u32[]{:S(2)}) collective-permute-start(bf16[128,256]{1,0:T(8,128)(2,1)} %slice.92), channel_id=1, source_target_pairs={{0,128},{4,132},{8,136},{12,140},{16,144},{20,148},{24,152},{28,15... | collective-permute-start | bytes 196616 | tf_op jit(solution)/shard_map/ppermute | solution.py:13
  15.1 2.9 collective-permute-start.4
  18.0 9.4 %collective-permute-start.3 = (bf16[128,256]{1,0:T(8,128)(2,1)}, bf16[128,256]{1,0:T(8,128)(2,1)}, u32[]{:S(2)}, u32[]{:S(2)}) collective-permute-start(bf16[128,256]{1,0:T(8,128)(2,1)} %slice.92), channel_id=1, source_target_pairs={{0,32},{4,36},{8,40},{12,44},{16,48},{20,52},{24,56},{28,60},{32,6... | collective-permute-start | bytes 196616 | tf_op jit(solution)/shard_map/ppermute | solution.py:13
  27.4 3.7 %collective-permute-start.2 = (bf16[128,256]{1,0:T(8,128)(2,1)}, bf16[128,256]{1,0:T(8,128)(2,1)}, u32[]{:S(2)}, u32[]{:S(2)}) collective-permute-start(bf16[128,256]{1,0:T(8,128)(2,1)} %slice.92), channel_id=1, source_target_pairs={{0,16},{4,20},{8,24},{12,28},{16,32},{20,36},{24,40},{28,44},{32,4... | collective-permute-start | bytes 196616 | tf_op jit(solution)/shard_map/ppermute | solution.py:13
  33.1 4.3 %collective-permute-start.6 = (bf16[128,256]{0,1:T(8,128)(2,1)}, bf16[128,256]{0,1:T(8,128)(2,1)}, u32[]{:S(2)}, u32[]{:S(2)}) collective-permute-start(bf16[128,256]{0,1:T(8,128)(2,1)} %slice.114), channel_id=1, source_target_pairs={{0,4},{4,8},{8,12},{12,16},{16,20},{20,24},{24,28},{28,32},{32,36}... | collective-permute-start | bytes 196616 | tf_op jit(solution)/shard_map/ppermute | solution.py:13
  39.2 2.8 pad_add_fusion
  44.9 5.3 %collective-permute-start = (bf16[128,256]{1,0:T(8,128)(2,1)}, bf16[128,256]{1,0:T(8,128)(2,1)S(1)}, u32[]{:S(2)}, u32[]{:S(2)}) collective-permute-start(bf16[128,256]{1,0:T(8,128)(2,1)} %slice.92), channel_id=1, source_target_pairs={{0,4},{4,8},{8,12},{12,16},{16,20},{20,24},{24,28},{28,32},{32,36}... | collective-permute-start | bytes 196616 | tf_op jit(solution)/shard_map/ppermute | solution.py:13
  55.2 6.1 %collective-permute-start.11 = (bf16[128,256]{0,1:T(8,128)(2,1)}, bf16[128,256]{0,1:T(8,128)(2,1)S(1)}, u32[]{:S(2)}, u32[]{:S(2)}) collective-permute-start(bf16[128,256]{0,1:T(8,128)(2,1)} %slice.114), channel_id=1, source_target_pairs={{0,128},{4,132},{8,136},{12,140},{16,144},{20,148},{24,152},{28,15... | collective-permute-start | bytes 196616 | tf_op jit(solution)/shard_map/ppermute | solution.py:13
  66.2 3.7 %collective-permute-start.8 = (bf16[128,256]{0,1:T(8,128)(2,1)}, bf16[128,256]{0,1:T(8,128)(2,1)S(1)}, u32[]{:S(2)}, u32[]{:S(2)}) collective-permute-start(bf16[128,256]{0,1:T(8,128)(2,1)} %slice.114), channel_id=1, source_target_pairs={{0,16},{4,20},{8,24},{12,28},{16,32},{20,36},{24,40},{28,44},{32,4... | collective-permute-start | bytes 196616 | tf_op jit(solution)/shard_map/ppermute | solution.py:13
  73.2 10.5 %fusion.27 = (f32[2,1024]{1,0:T(2,128)S(1)}, f32[2,1024,1792]{1,2,0:T(8,128)}) fusion(pred[1024,1792]{0,1:T(8,128)(4,1)} %pad_add_fusion, bf16[1792,2,128]{0,2,1:T(8,128)(2,1)S(1)} %bitcast.61, bf16[1024,2,128]{0,2,1:T(8,128)(2,1)S(1)} %bitcast.68), kind=kOutput, calls=%fused_computation.60 | convolution fusion | flops 954205952 | bytes 17965056 | tf_op jit(solution)/shard_map/sub | solution.py:45
  83.7 7.1 %fusion.16 = bf16[2,128,1024]{2,1,0:T(8,128)(2,1)} fusion(bf16[1792,2,128]{0,2,1:T(8,128)(2,1)S(1)} %bitcast.72, f32[2,1024,1792]{1,2,0:T(8,128)} %get-tuple-element.28, f32[2,1024]{1,0:T(2,128)S(1)} %get-tuple-element.27), kind=kOutput, calls=%fused_computation.23 | convolution fusion | flops 947126272 | bytes 16130048 | tf_op jit(solution)/shard_map/hqk,khd->qhd/dot_general | solution.py:48
  90.8 3.6 %fusion.30 = f32[256,1024]{1,0:T(8,128)} fusion(bf16[1024,256]{0,1:T(8,128)(2,1)} %bitcast.66, bf16[1024,1024]{1,0:T(8,128)(2,1)} %all-gather.2.cloned.1.call-done), kind=kOutput, calls=%fused_computation.63 | convolution fusion | flops 536870912 | bytes 3670016 | tf_op jit(solution)/shard_map/dot_general | solution.py:58
  94.6 3.1 convolution_convert_fusion
  98.6 9.4 %fusion.29 = (bf16[1792,2,128]{0,2,1:T(8,128)(2,1)S(1)}, f32[1792,2,128]{0,2,1:T(8,128)}) fusion(bf16[1024,2,128]{0,2,1:T(8,128)(2,1)S(1)} %bitcast.88, f32[2,1024,1792]{1,2,0:T(8,128)} %get-tuple-element.28, f32[2,1024]{1,0:T(2,128)S(1)} %get-tuple-element.27), kind=kOutput, calls=%fused_computation.62 | convolution fusion | flops 947322880 | bytes 17965056 | tf_op jit(solution)/shard_map/hqk,qhd->khd/dot_general | solution.py:66
  108.0 6.4 %multiply_reduce_fusion = (f32[2,1024]{1,0:T(2,128)S(1)}, f32[2,1024,1792]{1,2,0:T(8,128)}) fusion(f32[2,1024,1792]{1,2,0:T(8,128)S(1)} %bitcast.64, f32[2,1024]{1,0:T(2,128)S(1)} %get-tuple-element.27, bf16[1024,2,128]{0,2,1:T(8,128)(2,1)S(1)} %bitcast.89, bf16[1792,2,128]{0,2,1:T(8,128)(2,1)S(1)} %bitcast.73), kind=kOutput, calls=%fused_computation.3 | convolution fusion | flops 950532096 | bytes 30818304 | tf_op jit(solution)/shard_map/qhd,khd->hqk/dot_general | solution.py:65
  115.9 10.5 %multiply_convert_fusion = bf16[2,1024,1792]{1,2,0:T(8,128)(2,1)S(1)} fusion(f32[2,1024,1792]{1,2,0:T(8,128)} %get-tuple-element.30, f32[2,1024]{1,0:T(2,128)S(1)} %get-tuple-element.29, f32[2,1024,1792]{1,2,0:T(8,128)} %get-tuple-element.28, f32[2,1024]{1,0:T(2,128)S(1)} %get-tuple-element.27), kind=kLoop, calls=%fused_computation.2 | loop fusion | flops 14680064 | bytes 36716544 | tf_op jit(solution)/shard_map/convert_element_type | solution.py:70
  126.4 3.8 %fusion.28 = (bf16[1792,2,128]{0,2,1:T(8,128)(2,1)S(1)}, f32[1792,2,128]{0,2,1:T(8,128)}) fusion(bf16[2,1024,1792]{1,2,0:T(8,128)(2,1)S(1)} %multiply_convert_fusion, bf16[1024,2,128]{0,2,1:T(8,128)(2,1)S(1)} %bitcast.69), kind=kOutput, calls=%fused_computation.61 | convolution fusion | flops 940441600 | bytes 10616832 | tf_op jit(solution)/shard_map/hqk,qhd->khd/dot_general | solution.py:75
  140.3 5.4 %collective-permute-start.18 = (bf16[128,256]{1,0:T(8,128)(2,1)}, bf16[128,256]{1,0:T(8,128)(2,1)}, u32[]{:S(2)}, u32[]{:S(2)}) collective-permute-start(bf16[128,256]{1,0:T(8,128)(2,1)} %copy.61), channel_id=1, source_target_pairs={{4,0},{8,4},{12,8},{16,12},{20,16},{24,20},{28,24},{32,28},{36,32}... | collective-permute-start | bytes 196616 | tf_op jit(solution)/shard_map/ppermute | solution.py:13
  158.9 9.7 %collective-permute-start.12 = (bf16[128,256]{1,0:T(8,128)(2,1)S(1)}, bf16[128,256]{1,0:T(8,128)(2,1)S(1)}, u32[]{:S(2)}, u32[]{:S(2)}) collective-permute-start(bf16[128,256]{1,0:T(8,128)(2,1)S(1)} %copy.52), channel_id=1, source_target_pairs={{4,0},{8,4},{12,8},{16,12},{20,16},{24,20},{28,24},{32,28},{36,32}... | collective-permute-start | bytes 196616 | tf_op jit(solution)/shard_map/ppermute | solution.py:13
  171.7 3.7 %collective-permute-done.16 = bf16[128,256]{1,0:T(8,128)(2,1)S(1)} collective-permute-done((bf16[128,256]{1,0:T(8,128)(2,1)S(1)}, bf16[128,256]{1,0:T(8,128)(2,1)S(1)}, u32[]{:S(2)}, u32[]{:S(2)}) %collective-permute-start.16) | collective-permute-done | bytes 65568 | tf_op jit(solution)/shard_map/ppermute | solution.py:13
  175.4 8.5 %collective-permute-done.17 = bf16[128,256]{1,0:T(8,128)(2,1)S(1)} collective-permute-done((bf16[128,256]{1,0:T(8,128)(2,1)S(1)}, bf16[128,256]{1,0:T(8,128)(2,1)S(1)}, u32[]{:S(2)}, u32[]{:S(2)}) %collective-permute-start.17) | collective-permute-done | bytes 65568 | tf_op jit(solution)/shard_map/ppermute | solution.py:13
  184.8 102.1 %all-reduce.2.cloned.1.call-done = f32[256,1024]{1,0:T(8,128)} async-done(((f32[256,1024]{1,0:T(8,128)}), f32[256,1024]{1,0:T(8,128)}) %all-reduce.2.cloned.1.call-update) | async-done | bytes 1048592 | tf_op jit(solution)/shard_map/psum | solution.py:63
  286.9 34.7 %reduce-scatter.2.cloned.1.call-done = bf16[1024,256]{1,0:T(8,128)(2,1)} async-done(((bf16[1024,1024]{1,0:T(8,128)(2,1)}), bf16[1024,256]{1,0:T(8,128)(2,1)}) %reduce-scatter.2.cloned.1.call-update) | async-done | bytes 524304 | tf_op jit(solution)/shard_map/reduce_scatter | solution.py:51
  321.6 2.3 copy.92
  (122 shorter events, 50.7 us)
Async XLA Ops:
  7.2 83.6 %all-gather.2.cloned.1.call-start = ((), (), s32[]{:S(2)}) async-start(), calls=%async_computation.2 | async-start | bytes 2621440 | tf_op jit(solution)/shard_map/all_gather | solution.py:54
  8.8 62.1 %collective-permute-start.5 = (bf16[128,256]{1,0:T(8,128)(2,1)}, bf16[128,256]{1,0:T(8,128)(2,1)}, u32[]{:S(2)}, u32[]{:S(2)}) collective-permute-start(bf16[128,256]{1,0:T(8,128)(2,1)} %slice.92), channel_id=1, source_target_pairs={{0,128},{4,132},{8,136},{12,140},{16,144},{20,148},{24,152},{28,15... | collective-permute-start | bytes 196616 | tf_op jit(solution)/shard_map/ppermute | solution.py:13
  15.1 51.2 %collective-permute-start.4 = (bf16[128,256]{1,0:T(8,128)(2,1)}, bf16[128,256]{1,0:T(8,128)(2,1)}, u32[]{:S(2)}, u32[]{:S(2)}) collective-permute-start(bf16[128,256]{1,0:T(8,128)(2,1)} %slice.92), channel_id=1, source_target_pairs={{0,64},{4,68},{8,72},{12,76},{16,80},{20,84},{24,88},{28,92},{32,9... | collective-permute-start | bytes 196616 | tf_op jit(solution)/shard_map/ppermute | solution.py:13
  18.0 46.1 %collective-permute-start.3 = (bf16[128,256]{1,0:T(8,128)(2,1)}, bf16[128,256]{1,0:T(8,128)(2,1)}, u32[]{:S(2)}, u32[]{:S(2)}) collective-permute-start(bf16[128,256]{1,0:T(8,128)(2,1)} %slice.92), channel_id=1, source_target_pairs={{0,32},{4,36},{8,40},{12,44},{16,48},{20,52},{24,56},{28,60},{32,6... | collective-permute-start | bytes 196616 | tf_op jit(solution)/shard_map/ppermute | solution.py:13
  27.4 33.9 %collective-permute-start.2 = (bf16[128,256]{1,0:T(8,128)(2,1)}, bf16[128,256]{1,0:T(8,128)(2,1)}, u32[]{:S(2)}, u32[]{:S(2)}) collective-permute-start(bf16[128,256]{1,0:T(8,128)(2,1)} %slice.92), channel_id=1, source_target_pairs={{0,16},{4,20},{8,24},{12,28},{16,32},{20,36},{24,40},{28,44},{32,4... | collective-permute-start | bytes 196616 | tf_op jit(solution)/shard_map/ppermute | solution.py:13
  31.1 255.7 %all-reduce.2.cloned.1.call-start = ((), (), s32[]{:S(2)}) async-start(), calls=%async_computation.3 | async-start | bytes 2097152 | tf_op jit(solution)/shard_map/psum | solution.py:63
  33.1 8.9 %collective-permute-start.6 = (bf16[128,256]{0,1:T(8,128)(2,1)}, bf16[128,256]{0,1:T(8,128)(2,1)}, u32[]{:S(2)}, u32[]{:S(2)}) collective-permute-start(bf16[128,256]{0,1:T(8,128)(2,1)} %slice.114), channel_id=1, source_target_pairs={{0,4},{4,8},{8,12},{12,16},{16,20},{20,24},{24,28},{28,32},{32,36}... | collective-permute-start | bytes 196616 | tf_op jit(solution)/shard_map/ppermute | solution.py:13
  44.9 7.0 %collective-permute-start = (bf16[128,256]{1,0:T(8,128)(2,1)}, bf16[128,256]{1,0:T(8,128)(2,1)S(1)}, u32[]{:S(2)}, u32[]{:S(2)}) collective-permute-start(bf16[128,256]{1,0:T(8,128)(2,1)} %slice.92), channel_id=1, source_target_pairs={{0,4},{4,8},{8,12},{12,16},{16,20},{20,24},{24,28},{28,32},{32,36}... | collective-permute-start | bytes 196616 | tf_op jit(solution)/shard_map/ppermute | solution.py:13
  55.2 18.0 %collective-permute-start.11 = (bf16[128,256]{0,1:T(8,128)(2,1)}, bf16[128,256]{0,1:T(8,128)(2,1)S(1)}, u32[]{:S(2)}, u32[]{:S(2)}) collective-permute-start(bf16[128,256]{0,1:T(8,128)(2,1)} %slice.114), channel_id=1, source_target_pairs={{0,128},{4,132},{8,136},{12,140},{16,144},{20,148},{24,152},{28,15... | collective-permute-start | bytes 196616 | tf_op jit(solution)/shard_map/ppermute | solution.py:13
  61.3 11.8 %collective-permute-start.10 = (bf16[128,256]{0,1:T(8,128)(2,1)}, bf16[128,256]{0,1:T(8,128)(2,1)S(1)}, u32[]{:S(2)}, u32[]{:S(2)}) collective-permute-start(bf16[128,256]{0,1:T(8,128)(2,1)} %slice.114), channel_id=1, source_target_pairs={{0,64},{4,68},{8,72},{12,76},{16,80},{20,84},{24,88},{28,92},{32,9... | collective-permute-start | bytes 196616 | tf_op jit(solution)/shard_map/ppermute | solution.py:13
  64.1 9.0 %collective-permute-start.9 = (bf16[128,256]{0,1:T(8,128)(2,1)}, bf16[128,256]{0,1:T(8,128)(2,1)S(1)}, u32[]{:S(2)}, u32[]{:S(2)}) collective-permute-start(bf16[128,256]{0,1:T(8,128)(2,1)} %slice.114), channel_id=1, source_target_pairs={{0,32},{4,36},{8,40},{12,44},{16,48},{20,52},{24,56},{28,60},{32,6... | collective-permute-start | bytes 196616 | tf_op jit(solution)/shard_map/ppermute | solution.py:13
  94.4 227.2 %reduce-scatter.2.cloned.1.call-start = ((), (), s32[]{:S(2)}) async-start(), calls=%async_computation.1 | async-start | bytes 2621440 | tf_op jit(solution)/shard_map/reduce_scatter | solution.py:51
  114.6 25.7 %collective-permute-start.19 = (bf16[128,256]{1,0:T(8,128)(2,1)S(1)}, bf16[128,256]{1,0:T(8,128)(2,1)S(1)}, u32[]{:S(2)}, u32[]{:S(2)}) collective-permute-start(bf16[128,256]{1,0:T(8,128)(2,1)S(1)} %copy.63), channel_id=1, source_target_pairs={{8,0},{12,4},{16,8},{20,12},{24,16},{28,20},{32,24},{36,28},{40,32... | collective-permute-start | bytes 196616 | tf_op jit(solution)/shard_map/ppermute | solution.py:13
  135.1 16.0 %collective-permute-start.20 = (bf16[128,256]{1,0:T(8,128)(2,1)}, bf16[128,256]{1,0:T(8,128)(2,1)S(1)}, u32[]{:S(2)}, u32[]{:S(2)}) collective-permute-start(bf16[128,256]{1,0:T(8,128)(2,1)} %copy.64), channel_id=1, source_target_pairs={{16,0},{20,4},{24,8},{28,12},{32,16},{36,20},{40,24},{44,28},{48,3... | collective-permute-start | bytes 196616 | tf_op jit(solution)/shard_map/ppermute | solution.py:13
  136.4 16.0 %collective-permute-start.21 = (bf16[128,256]{1,0:T(8,128)(2,1)}, bf16[128,256]{1,0:T(8,128)(2,1)S(1)}, u32[]{:S(2)}, u32[]{:S(2)}) collective-permute-start(bf16[128,256]{1,0:T(8,128)(2,1)} %copy.65), channel_id=1, source_target_pairs={{32,0},{36,4},{40,8},{44,12},{48,16},{52,20},{56,24},{60,28},{64,3... | collective-permute-start | bytes 196616 | tf_op jit(solution)/shard_map/ppermute | solution.py:13
  137.7 16.0 %collective-permute-start.22 = (bf16[128,256]{1,0:T(8,128)(2,1)}, bf16[128,256]{1,0:T(8,128)(2,1)S(1)}, u32[]{:S(2)}, u32[]{:S(2)}) collective-permute-start(bf16[128,256]{1,0:T(8,128)(2,1)} %copy.66), channel_id=1, source_target_pairs={{64,0},{68,4},{72,8},{76,12},{80,16},{84,20},{88,24},{92,28},{96,3... | collective-permute-start | bytes 196616 | tf_op jit(solution)/shard_map/ppermute | solution.py:13
  139.0 16.3 %collective-permute-start.23 = (bf16[128,256]{1,0:T(8,128)(2,1)}, bf16[128,256]{1,0:T(8,128)(2,1)}, u32[]{:S(2)}, u32[]{:S(2)}) collective-permute-start(bf16[128,256]{1,0:T(8,128)(2,1)} %copy.67), channel_id=1, source_target_pairs={{128,0},{132,4},{136,8},{140,12},{144,16},{148,20},{152,24},{156,2... | collective-permute-start | bytes 196616 | tf_op jit(solution)/shard_map/ppermute | solution.py:13
  140.3 16.3 %collective-permute-start.18 = (bf16[128,256]{1,0:T(8,128)(2,1)}, bf16[128,256]{1,0:T(8,128)(2,1)}, u32[]{:S(2)}, u32[]{:S(2)}) collective-permute-start(bf16[128,256]{1,0:T(8,128)(2,1)} %copy.61), channel_id=1, source_target_pairs={{4,0},{8,4},{12,8},{16,12},{20,16},{24,20},{28,24},{32,28},{36,32}... | collective-permute-start | bytes 196616 | tf_op jit(solution)/shard_map/ppermute | solution.py:13
  151.1 7.8 %collective-permute-start.13 = (bf16[128,256]{1,0:T(8,128)(2,1)S(1)}, bf16[128,256]{1,0:T(8,128)(2,1)S(1)}, u32[]{:S(2)}, u32[]{:S(2)}) collective-permute-start(bf16[128,256]{1,0:T(8,128)(2,1)S(1)} %copy.54), channel_id=1, source_target_pairs={{8,0},{12,4},{16,8},{20,12},{24,16},{28,20},{32,24},{36,28},{40,32... | collective-permute-start | bytes 196616 | tf_op jit(solution)/shard_map/ppermute | solution.py:13
  152.4 17.0 %collective-permute-start.14 = (bf16[128,256]{1,0:T(8,128)(2,1)S(1)}, bf16[128,256]{1,0:T(8,128)(2,1)S(1)}, u32[]{:S(2)}, u32[]{:S(2)}) collective-permute-start(bf16[128,256]{1,0:T(8,128)(2,1)S(1)} %copy.55), channel_id=1, source_target_pairs={{16,0},{20,4},{24,8},{28,12},{32,16},{36,20},{40,24},{44,28},{48,3... | collective-permute-start | bytes 196616 | tf_op jit(solution)/shard_map/ppermute | solution.py:13
  153.7 18.0 %collective-permute-start.15 = (bf16[128,256]{1,0:T(8,128)(2,1)S(1)}, bf16[128,256]{1,0:T(8,128)(2,1)S(1)}, u32[]{:S(2)}, u32[]{:S(2)}) collective-permute-start(bf16[128,256]{1,0:T(8,128)(2,1)S(1)} %copy.56), channel_id=1, source_target_pairs={{32,0},{36,4},{40,8},{44,12},{48,16},{52,20},{56,24},{60,28},{64,3... | collective-permute-start | bytes 196616 | tf_op jit(solution)/shard_map/ppermute | solution.py:13
  155.3 20.1 %collective-permute-start.16 = (bf16[128,256]{1,0:T(8,128)(2,1)S(1)}, bf16[128,256]{1,0:T(8,128)(2,1)S(1)}, u32[]{:S(2)}, u32[]{:S(2)}) collective-permute-start(bf16[128,256]{1,0:T(8,128)(2,1)S(1)} %copy.57), channel_id=1, source_target_pairs={{64,0},{68,4},{72,8},{76,12},{80,16},{84,20},{88,24},{92,28},{96,3... | collective-permute-start | bytes 196616 | tf_op jit(solution)/shard_map/ppermute | solution.py:13
  156.6 27.3 %collective-permute-start.17 = (bf16[128,256]{1,0:T(8,128)(2,1)S(1)}, bf16[128,256]{1,0:T(8,128)(2,1)S(1)}, u32[]{:S(2)}, u32[]{:S(2)}) collective-permute-start(bf16[128,256]{1,0:T(8,128)(2,1)S(1)} %copy.58), channel_id=1, source_target_pairs={{128,0},{132,4},{136,8},{140,12},{144,16},{148,20},{152,24},{156,2... | collective-permute-start | bytes 196616 | tf_op jit(solution)/shard_map/ppermute | solution.py:13
  158.9 25.0 %collective-permute-start.12 = (bf16[128,256]{1,0:T(8,128)(2,1)S(1)}, bf16[128,256]{1,0:T(8,128)(2,1)S(1)}, u32[]{:S(2)}, u32[]{:S(2)}) collective-permute-start(bf16[128,256]{1,0:T(8,128)(2,1)S(1)} %copy.52), channel_id=1, source_target_pairs={{4,0},{8,4},{12,8},{16,12},{20,16},{24,20},{28,24},{32,28},{36,32}... | collective-permute-start | bytes 196616 | tf_op jit(solution)/shard_map/ppermute | solution.py:13
  (16 other events, 455.5 us)
Sparse Core Ops, SparseCore 0:
  31.2 31.4 all-gather.1
  94.5 192.3 all-reduce.1
  290.2 31.3 reduce-scatter.1
where the time goes:
time: 332 us; the launch traced here: 330 us
  waiting for transfers between devices  156 us (47%)
  starting transfers between devices  76.2 us (23%)
  matrix products  45.8 us (14%)
  local copies, waits for them, and re-layouts  22.1 us (7%)
  other arithmetic  16.2 us (5%)
  between operations  14.4 us (4%)
    psum x1, waiting for transfers between devices, local(): weight_grad = lax.psum(grad_weight, 'seq')  102 us
    ppermute x24, starting transfers between devices, from_behind(): return lax.ppermute(x, axis, pairs)  75.9 us
    reduce_scatter x1, waiting for transfers between devices, local(): lax.psum_scatter(partial_out.astype(jnp.bfloat16), 'head', scatter_dimens...  34.7 us
    ppermute x24, waiting for transfers between devices, from_behind(): return lax.ppermute(x, axis, pairs)  18.8 us
    convert_element_type x1, other arithmetic, local(): dscore = (prob * (dprob - delta)).astype(jnp.bfloat16)  10.5 us
    sub x1, matrix products, local(): expo = jnp.exp(scores - top)  10.5 us
    dot_general x1, matrix products, local(): jnp.einsum('hqk,qhd->khd', prob_low, dattn_three, preferred_element_type=...  9.35 us
    unnamed x41, local copies, waits for them, and re-layouts  8.18 us
  transfers between devices with their start and end apart: 27, of which 9 were waited for; matrix products, arithmetic and copies ran while one was open for 23% of the time, Pallas kernels for 0%

commit v1 on v0

v1 whole, which is shorter than its diff:
```python
import functools

import jax
import jax.numpy as jnp
import numpy as np
from jax import lax
from jax.experimental import pallas as pl
from jax.experimental.pallas import tpu as pltpu
from jax.sharding import PartitionSpec as P

TILE = 128
DH = 128
STEP = 256
MESH = pl.DeviceIdType.MESH
F32 = jnp.float32
BF16 = jnp.bfloat16
NEG = -1e30
FAR = 3e38


def mm(a, b):
    return jnp.dot(a, b, preferred_element_type=F32)


def mm_t(a, b):
    return lax.dot_general(a, b, (((1,), (1,)), ((), ())), preferred_element_type=F32)


def kernel(
    plan,
    q_ref, k_ref, v_ref, w_ref, c_ref,
    out_ref, dq_ref, dk_ref, dv_ref, wg_ref,
    ktile, vtile, kback, vback, ksend, vsend,
    cot, kt, vt, ktt, vtt,
    s_own, s_tile, e_own, e_tile, d_own, d_tile,
    acc, attn_t32, attn_t, attn, m_o, l_o, m_t, r_o, r_t, del_o, del_t,
    datt_t, datt_o, datt_s, datt_on, datt_sn, dqt,
    p_send, p_own, p_from,
    g_send, g_from, g_part, g_ysend, g_yfrom, g_y, g_zsend, g_zfrom, g_full,
    fwd_s, fwd_r, bwd_s, bwd_r, x_s, x_r, w_s, w_r,
):
    seq, heads_x, levels, ny, nz, ystride = plan
    rows, width = q_ref.shape
    nh = width // DH
    nb = rows // STEP
    tail = rows - TILE
    b = lax.axis_index("seq")
    x = lax.axis_index("head")
    core = lax.rem(b, 2)
    yy = b // ystride
    zz = lax.rem(b, ystride) // 2
    right = lax.rem(x + 1, heads_x)
    left = lax.rem(x + heads_x - 1, heads_x)
    over = lax.rem(x + 2, heads_x)
    factor = float(DH ** (-0.5) * np.log2(np.e))
    scale = DH ** (-0.5)

    def ahead(l):
        return (lax.rem(b + 2**l, seq), x)

    def behind(l):
        return (lax.rem(b + seq - 2**l, seq), x)

    sibling = (b + 1 - 2 * core, x)

    def ypeer(d):
        return lax.rem(yy + d, ny)

    def zpeer(d):
        return lax.rem(zz + d, nz)

    def yid(d):
        return (ypeer(d) * ystride + zz * 2 + core, x)

    def zid(d):
        return (yy * ystride + zpeer(d) * 2 + core, x)

    peers = [ahead(l) for l in range(levels)] + [behind(l) for l in range(levels)]
    peers += [sibling] + [yid(d) for d in range(1, ny)] + [zid(d) for d in range(1, nz)]
    peers += [(b, right), (b, left), (b, over)]
    barrier = pltpu.get_barrier_semaphore()
    for peer in peers:
        pl.semaphore_signal(barrier, inc=1, device_id=peer, device_id_type=MESH)

    def remote(src, dst, sems, semr, idx, to):
        c = pltpu.make_async_remote_copy(
            src_ref=src, dst_ref=dst, send_sem=sems.at[idx], recv_sem=semr.at[idx],
            device_id=to, device_id_type=MESH,
        )
        c.start()
        return c

    def hs(h):
        return pl.ds(pl.multiple_of(h * DH, DH), DH)

    kt[...] = k_ref[...].T
    vt[...] = v_ref[...].T
    pl.semaphore_wait(barrier, len(peers))

    sent = []
    order = list(range(levels))[::-1]
    ktc, vtc = {}, {}
    for l in order:
        span = pl.ds(l * TILE, TILE)
        ktc[l] = remote(k_ref.at[pl.ds(tail, TILE)], ktile.at[span], fwd_s, fwd_r, 2 * l, ahead(l))
        vtc[l] = remote(v_ref.at[pl.ds(tail, TILE)], vtile.at[span], fwd_s, fwd_r, 2 * l + 1, ahead(l))
        sent += [ktc[l], vtc[l]]

    half = rows // 2
    lo, hi = pl.ds(0, half), pl.ds(half, half)
    mine = cot.at[x]
    to_right_lo = remote(c_ref.at[lo], mine.at[lo], x_s, x_r, 0, (b, right))
    to_left_hi = remote(c_ref.at[hi], mine.at[hi], x_s, x_r, 1, (b, left))
    to_right_hi = remote(c_ref.at[hi], mine.at[hi], x_s, x_r, 2, (b, right))
    to_left_lo = remote(c_ref.at[lo], mine.at[lo], x_s, x_r, 3, (b, left))
    sent += [to_right_lo, to_left_hi, to_right_hi, to_left_lo]

    def own_fwd(h, _):
        for i in range(nb):
            cols = pl.ds(i * STEP, STEP)
            qi = q_ref[cols, hs(h)]
            top = jnp.full((1, STEP), NEG, F32)
            for j in range(i + 1):
                s = mm_t(k_ref[pl.ds(j * STEP, STEP), hs(h)], qi)
                if j == i:
                    key = lax.broadcasted_iota(jnp.int32, (STEP, STEP), 0)
                    query = lax.broadcasted_iota(jnp.int32, (STEP, STEP), 1)
                    s = jnp.where(key <= query, s, NEG)
                s_own[pl.ds(j * STEP, STEP), :] = s
                top = jnp.maximum(top, jnp.max(s, axis=0, keepdims=True))
            m_o[h, :, cols] = top
            total = jnp.zeros((1, STEP), F32)
            part = jnp.zeros((DH, STEP), F32)
            for j in range(i + 1):
                e = jnp.exp2((s_own[pl.ds(j * STEP, STEP), :] - top) * factor)
                total = total + jnp.sum(e, axis=0, keepdims=True)
                e = e.astype(BF16)
                e_own[h, pl.ds(j * STEP, STEP), cols] = e
                part = part + mm(vt[hs(h), pl.ds(j * STEP, STEP)], e)
            l_o[h, :, cols] = total
            acc[hs(h), cols] = part
        return 0

    lax.fori_loop(0, nh, own_fwd, 0)

    cot[x] = c_ref[...]
    to_right_lo.wait_recv()
    pass_lo = remote(cot.at[left, lo], cot.at[left, lo], x_s, x_r, 4, (b, right))
    to_left_hi.wait_recv()
    pass_hi = remote(cot.at[right, hi], cot.at[right, hi], x_s, x_r, 5, (b, left))
    sent += [pass_lo, pass_hi]

    for h in range(nh):
        m_t[h] = jnp.full((1, rows), NEG, F32)
    valid = {l: b >= 2**l for l in range(levels)}
    for l in order:
        span = pl.ds(l * TILE, TILE)
        ktc[l].wait_recv()
        vtc[l].wait_recv()

        def tile_scores(h, _):
            for i in range(nb):
                cols = pl.ds(i * STEP, STEP)
                s = mm_t(ktile[span, hs(h)], q_ref[cols, hs(h)])
                s_tile[h, span, cols] = s
                top = jnp.max(s, axis=0, keepdims=True)
                m_t[h, :, cols] = jnp.maximum(m_t[h, :, cols], jnp.where(valid[l], top, NEG))
            return 0

        lax.fori_loop(0, nh, tile_scores, 0)
        ktt[:, span] = ktile[span, :].T
        vtt[:, span] = vtile[span, :].T

    def tile_fwd(h, _):
        for i in range(nb):
            cols = pl.ds(i * STEP, STEP)
            top = m_t[h, :, cols]
            total = jnp.zeros((1, STEP), F32)
            part = jnp.zeros((DH, STEP), F32)
            for l in range(levels):
                span = pl.ds(l * TILE, TILE)
                shift = jnp.where(valid[l], top, FAR)
                e = jnp.exp2((s_tile[h, span, cols] - shift) * factor)
                total = total + jnp.sum(e, axis=0, keepdims=True)
                e_tile[h, span, cols] = e.astype(BF16)
            part = mm(vtt[hs(h), :], e_tile[h, :, cols])
            mo = m_o[h, :, cols]
            m = jnp.maximum(mo, top)
            fo = jnp.exp2((mo - m) * factor)
            ft = jnp.exp2((top - m) * factor)
            inv = 1.0 / (fo * l_o[h, :, cols] + ft * total)
            fo = fo * inv
            ft = ft * inv
            r_o[h, :, cols] = fo
            r_t[h, :, cols] = ft
            at = acc[hs(h), cols] * fo + part * ft
            attn_t32[hs(h), cols] = at
            attn_t[hs(h), cols] = at.astype(BF16)
            attn[cols, hs(h)] = at.T.astype(BF16)
        return 0

    lax.fori_loop(0, nh, tile_fwd, 0)

    def wcols(at):
        return pl.ds(pl.multiple_of(at * width, width), width)

    p_send[0] = mm(attn[...], w_ref[:, wcols(over)]).astype(BF16)
    o_lo = remote(p_send.at[0, lo], p_from.at[0, lo], x_s, x_r, 6, (b, right))
    o_hi = remote(p_send.at[0, hi], p_from.at[1, hi], x_s, x_r, 7, (b, left))
    p_send[1] = mm(attn[...], w_ref[:, wcols(right)]).astype(BF16)
    r_hi = remote(p_send.at[1, hi], p_from.at[2, hi], x_s, x_r, 8, (b, right))
    p_send[2] = mm(attn[...], w_ref[:, wcols(left)]).astype(BF16)
    l_lo = remote(p_send.at[2, lo], p_from.at[3, lo], x_s, x_r, 9, (b, left))
    sent += [o_lo, o_hi, r_hi, l_lo]
    p_own[...] = mm(attn[...], w_ref[:, wcols(x)])

    to_right_hi.wait_recv()
    to_left_lo.wait_recv()
    pass_lo.wait_recv()
    pass_hi.wait_recv()

    for i in range(nb):
        cols = pl.ds(i * STEP, STEP)
        g = jnp.zeros((width, STEP), F32)
        for j in range(heads_x):
            g = g + mm_t(w_ref[:, pl.ds(j * width, width)], cot[j, cols, :])
        datt_t[:, cols] = g.astype(BF16)

    def spread(h, _):
        for i in range(nb):
            cols = pl.ds(i * STEP, STEP)
            g = datt_t[hs(h), cols].astype(F32)
            at = attn_t32[hs(h), cols]
            go = (g * r_o[h, :, cols]).astype(BF16)
            gt = (g * r_t[h, :, cols]).astype(BF16)
            datt_o[hs(h), cols] = go
            datt_s[hs(h), cols] = gt
            go = go.astype(F32)
            gt = gt.astype(F32)
            del_o[h, :, cols] = jnp.sum(go * at, axis=0, keepdims=True)
            del_t[h, :, cols] = jnp.sum(gt * at, axis=0, keepdims=True)
            datt_on[cols, hs(h)] = go.T.astype(BF16)
            datt_sn[cols, hs(h)] = gt.T.astype(BF16)
        return 0

    lax.fori_loop(0, nh, spread, 0)

    gh = width // 2
    for j in range(heads_x):
        g_send[:, pl.ds(j * width, width)] = mm(
            attn_t[pl.ds(pl.multiple_of((1 - core) * gh, gh), gh), :], cot[j]
        ).astype(BF16)
    g_core = remote(g_send, g_from, w_s, w_r, 0, sibling)
    sent.append(g_core)
    for j in range(heads_x):
        g_part[:, pl.ds(j * width, width)] = mm(
            attn_t[pl.ds(pl.multiple_of(core * gh, gh), gh), :], cot[j]
        )

    kbc, vbc = {}, {}

    def tile_bwd_for(l):
        span = pl.ds(l * TILE, TILE)

        def tile_bwd(h, _):
            for i in range(nb):
                cols = pl.ds(i * STEP, STEP)
                dp = mm(vtile[span, hs(h)], datt_s[hs(h), cols])
                d = e_tile[h, span, cols].astype(F32) * (dp - del_t[h, :, cols])
                d_tile[h, span, cols] = d.astype(BF16)
            ksend[span, hs(h)] = (mm(d_tile[h, span, :], q_ref[:, hs(h)]) * scale).astype(BF16)
            vsend[span, hs(h)] = mm(e_tile[h, span, :], datt_sn[:, hs(h)]).astype(BF16)
            return 0

        lax.fori_loop(0, nh, tile_bwd, 0)
        kbc[l] = remote(ksend.at[span], kback.at[span], bwd_s, bwd_r, 2 * l, behind(l))
        vbc[l] = remote(vsend.at[span], vback.at[span], bwd_s, bwd_r, 2 * l + 1, behind(l))

    for l in order[: levels // 2]:
        tile_bwd_for(l)

    gy = gh // ny
    g_core.wait_recv()
    g_part[...] = g_part[...] + g_from[...].astype(F32)
    g_ysend[...] = g_part[...].astype(BF16)

    def yrows(at):
        return pl.ds(pl.multiple_of(at * gy, gy), gy)

    ysum = [
        remote(g_ysend.at[yrows(ypeer(d))], g_yfrom.at[d], w_s, w_r, d, yid(d)) for d in range(1, ny)
    ]
    sent += ysum

    for l in order[levels // 2 :]:
        tile_bwd_for(l)
    for l in order:
        sent += [kbc[l], vbc[l]]

    o_lo.wait_recv()
    p_send[1, lo, :] = (p_send[1, lo, :].astype(F32) + p_from[0, lo, :].astype(F32)).astype(BF16)
    pass_r = remote(p_send.at[1, lo], p_from.at[2, lo], x_s, x_r, 10, (b, right))
    o_hi.wait_recv()
    p_send[2, hi, :] = (p_send[2, hi, :].astype(F32) + p_from[1, hi, :].astype(F32)).astype(BF16)
    pass_l = remote(p_send.at[2, hi], p_from.at[3, hi], x_s, x_r, 11, (b, left))
    sent += [pass_r, pass_l]

    gz = heads_x * width // nz

    def zcols(at):
        return pl.ds(pl.multiple_of(at * gz, gz), gz)

    for c in ysum:
        c.wait_recv()
    total = g_part[yrows(yy), :]
    for d in range(1, ny):
        total = total + g_yfrom[d].astype(F32)
    g_y[...] = total
    g_zsend[...] = total.astype(BF16)
    zsum = [
        remote(g_zsend.at[:, zcols(zpeer(d))], g_zfrom.at[d], w_s, w_r, ny + d, zid(d))
        for d in range(1, nz)
    ]
    sent += zsum

    def own_bwd(h, _):
        for j in range(nb):
            span = pl.ds(j * STEP, STEP)
            for i in range(j, nb):
                cols = pl.ds(i * STEP, STEP)
                dp = mm(v_ref[span, hs(h)], datt_o[hs(h), cols])
                d = e_own[h, span, cols].astype(F32) * (dp - del_o[h, :, cols])
                d_own[h, span, cols] = d.astype(BF16)
            rest = pl.ds(j * STEP, rows - j * STEP)
            dk = mm(d_own[h, span, rest], q_ref[rest, hs(h)]) * scale
            dv = mm(e_own[h, span, rest], datt_on[rest, hs(h)])
            dk_ref[span, hs(h)] = dk.astype(BF16)
            dv_ref[span, hs(h)] = dv.astype(BF16)
            if j == nb - 1:
                dqt[0, :, hs(h)] = dk[STEP - TILE :]
                dqt[1, :, hs(h)] = dv[STEP - TILE :]
        for i in range(nb):
            cols = pl.ds(i * STEP, STEP)
            upto = pl.ds(0, (i + 1) * STEP)
            g = mm(kt[hs(h), upto], d_own[h, upto, cols])
            g = g + mm(ktt[hs(h), :], d_tile[h, :, cols])
            dq_ref[cols, hs(h)] = (g * scale).T.astype(BF16)
        return 0

    own_bwd(0, 0)

    for c in zsum:
        c.wait_recv()
    piece = g_y[:, zcols(zz)]
    for d in range(1, nz):
        piece = piece + g_zfrom[d].astype(F32)
    at_rows = pl.ds(pl.multiple_of(core * gh + yy * gy, gy), gy)
    g_full[at_rows, zcols(zz)] = piece.astype(BF16)
    zall = [
        remote(g_full.at[at_rows, zcols(zz)], g_full.at[at_rows, zcols(zz)], w_s, w_r, ny + nz + d, zid(d))
        for d in range(1, nz)
    ]
    sent += zall

    for h in range(1, nh):
        own_bwd(h, 0)

    for c in zall:
        c.wait_recv()
    yall = [
        remote(g_full.at[at_rows], g_full.at[at_rows], w_s, w_r, ny + 2 * nz + d, yid(d))
        for d in range(1, ny)
    ]
    sent += yall

    r_hi.wait_recv()
    l_lo.wait_recv()
    pass_r.wait_recv()
    pass_l.wait_recv()
    out_ref[...] = (p_own[...] + p_from[2].astype(F32) + p_from[3].astype(F32)).astype(BF16)

    for c in yall:
        c.wait_recv()
    core_rows = pl.ds(pl.multiple_of(core * gh, gh), gh)
    g_last = remote(g_full.at[core_rows], g_full.at[core_rows], w_s, w_r, 2 * ny + 2 * nz, sibling)
    sent.append(g_last)

    dk = dqt[0]
    dv = dqt[1]
    for l in order:
        span = pl.ds(l * TILE, TILE)
        kbc[l].wait_recv()
        vbc[l].wait_recv()
        dk = dk + kback[span, :].astype(F32)
        dv = dv + vback[span, :].astype(F32)
    dk_ref[pl.ds(tail, TILE), :] = dk.astype(BF16)
    dv_ref[pl.ds(tail, TILE), :] = dv.astype(BF16)

    g_last.wait_recv()
    wg_ref[...] = g_full[...].astype(F32)
    for c in sent:
        c.wait_send()


def local(plan, queries, keys, values, out_weight, cotangent):
    seq, heads_x, levels, ny, nz, _ = plan
    rows, width = queries.shape
    nh = width // DH
    far = levels * TILE
    wide = heads_x * width
    gh = width // 2
    gy = gh // ny
    gz = wide // nz
    dma = pltpu.SemaphoreType.DMA
    like = [(rows, width)] * 4
    return pl.pallas_call(
        functools.partial(kernel, plan),
        out_shape=[jax.ShapeDtypeStruct(s, BF16) for s in like]
        + [jax.ShapeDtypeStruct((width, wide), F32)],
        in_specs=[pl.BlockSpec(memory_space=pltpu.VMEM)] * 5,
        out_specs=[pl.BlockSpec(memory_space=pltpu.VMEM)] * 5,
        scratch_shapes=[
            pltpu.VMEM((far, width), BF16), pltpu.VMEM((far, width), BF16),
            pltpu.VMEM((far, width), BF16), pltpu.VMEM((far, width), BF16),
            pltpu.VMEM((far, width), BF16), pltpu.VMEM((far, width), BF16),
            pltpu.VMEM((heads_x, rows, width), BF16),
            pltpu.VMEM((width, rows), BF16), pltpu.VMEM((width, rows), BF16),
            pltpu.VMEM((width, far), BF16), pltpu.VMEM((width, far), BF16),
            pltpu.VMEM((rows, STEP), F32), pltpu.VMEM((nh, far, rows), F32),
            pltpu.VMEM((nh, rows, rows), BF16), pltpu.VMEM((nh, far, rows), BF16),
            pltpu.VMEM((nh, rows, rows), BF16), pltpu.VMEM((nh, far, rows), BF16),
            pltpu.VMEM((width, rows), F32), pltpu.VMEM((width, rows), F32),
            pltpu.VMEM((width, rows), BF16), pltpu.VMEM((rows, width), BF16),
        ]
        + [pltpu.VMEM((nh, 1, rows), F32)] * 7
        + [
            pltpu.VMEM((width, rows), BF16), pltpu.VMEM((width, rows), BF16),
            pltpu.VMEM((width, rows), BF16), pltpu.VMEM((rows, width), BF16),
            pltpu.VMEM((rows, width), BF16), pltpu.VMEM((2, TILE, width), F32),
            pltpu.VMEM((3, rows, width), BF16), pltpu.VMEM((rows, width), F32),
            pltpu.VMEM((4, rows, width), BF16),
            pltpu.VMEM((gh, wide), BF16), pltpu.VMEM((gh, wide), BF16),
            pltpu.VMEM((gh, wide), F32), pltpu.VMEM((gh, wide), BF16),
            pltpu.VMEM((ny, gy, wide), BF16), pltpu.VMEM((gy, wide), F32),
            pltpu.VMEM((gy, wide), BF16), pltpu.VMEM((nz, gy, gz), BF16),
            pltpu.VMEM((width, wide), BF16),
            dma((2 * levels,)), dma((2 * levels,)), dma((2 * levels,)), dma((2 * levels,)),
            dma((12,)), dma((12,)),
            dma((2 * ny + 2 * nz + 1,)), dma((2 * ny + 2 * nz + 1,)),
        ],
        compiler_params=pltpu.CompilerParams(
            collective_id=0, has_side_effects=True, vmem_limit_bytes=60 * 1024 * 1024
        ),
        name="layer",
    )(queries, keys, values, out_weight, cotangent)


def solution(mesh):
    seq = mesh.shape["seq"]
    heads_x = mesh.shape["head"]
    levels = seq.bit_length() - 1
    ny = 4 if seq >= 16 else 2
    ystride = seq // ny
    plan = (seq, heads_x, levels, ny, ystride // 2, ystride)
    return jax.shard_map(
        functools.partial(local, plan),
        mesh=mesh,
        in_specs=(
            P("seq", "head"), P("seq", "head"), P("seq", "head"), P("head", None), P("seq", "head"),
        ),
        out_specs=(
            P("seq", "head"), P("seq", "head"), P("seq", "head"), P("seq", "head"), P("head", None),
        ),
        check_vma=False,
    )
```

time: 332 us -> 78.4 us (0.24)
  waiting for transfers between devices: 156 us -> 0 us
  starting transfers between devices: 76.2 us -> 0 us
  Pallas kernels: 0 us -> 71.9 us
  matrix products: 45.8 us -> 0 us
  local copies, waits for them, and re-layouts: 22.1 us -> 5.72 us
  other arithmetic: 16.2 us -> 0 us
  between operations: 14.4 us -> 0.65 us
    psum x1 -> x0, waiting for transfers between devices: 102 us -> none  [local(): weight_grad = lax.psum(grad_weight, 'seq')]
    ppermute x24 -> x0, starting transfers between devices: 75.9 us -> none  [from_behind(): return lax.ppermute(x, axis, pairs)]
    pallas_call x0 -> x1, Pallas kernels: none -> 71.9 us  [local(): pl.pallas_call(functools.partial(kernel, plan), out_shape=[jax.ShapeDtype...]
    dot_general x8 -> x0, matrix products: 35.3 us -> none  [the longest x1 9.35 us: local(): jnp.einsum('hqk,qhd->khd', prob_low, dattn_three, preferred_element_type=...]
    reduce_scatter x1 -> x0, waiting for transfers between devices: 34.7 us -> none  [local(): lax.psum_scatter(partial_out.astype(jnp.bfloat16), 'head', scatter_dimens...]
    ppermute x24 -> x0, waiting for transfers between devices: 18.8 us -> none  [from_behind(): return lax.ppermute(x, axis, pairs)]
    convert_element_type x1 -> x0, other arithmetic: 10.5 us -> none  [local(): dscore = (prob * (dprob - delta)).astype(jnp.bfloat16)]
    sub x1 -> x0, matrix products: 10.5 us -> none  [local(): expo = jnp.exp(scores - top)]
  transfers between devices with their start and end apart: 27 -> 0, of which waited for: 9 -> 0; matrix products, arithmetic and copies ran while one was open for 23% -> 0% of each run, Pallas kernels for 0% -> 0%
where the time goes in v1:
time: 78.4 us; the launch traced here: 78.3 us
  Pallas kernels  71.9 us (92%)
  local copies, waits for them, and re-layouts  5.72 us (7%)
    pallas_call x1, Pallas kernels, local(): pl.pallas_call(functools.partial(kernel, plan), out_shape=[jax.ShapeDtype...  71.9 us
    unnamed x13, local copies, waits for them, and re-layouts  5.72 us

profile of v1, /device:TPU:1, one launch (start us, length us, event | category | flops | bytes accessed | tf_op | source)
XLA Modules:
  0.0 78.3 jit_solution(3297814565340100524)
XLA Ops:
  0.6 71.9 %layer.1 = (bf16[1024,256]{1,0:T(8,128)(2,1)}, bf16[1024,256]{1,0:T(8,128)(2,1)}, bf16[1024,256]{1,0:T(8,128)(2,1)}, bf16[1024,256]{1,0:T(8,128)(2,1)}, f32[256,1024]{1,0:T(8,128)}) custom-call(bf16[1024,256]{1,0:T(8,128)(2,1)} %q_ref.1, bf16[1024,256]{1,0:T(8,128)(2,1)} %k_ref.1, bf16[1024,256]{1,0:T(8,128)(2,1)} %v_ref.1, bf16[256,1024]{1,0:T(8,128)(2,1)} %w_ref.1, ...), custom_call_target="tpu_custom_call" | custom-call | tf_op jit(solution)/shard_map/layer/pallas_call | solution.py:416
  72.5 0.0 copy-start.3
  72.5 1.9 %copy.15 = bf16[1024,256]{1,0:T(8,128)(2,1)} copy(bf16[1024,256]{1,0:T(8,128)(2,1)} %get-tuple-element.10) | data formatting | bytes 1048576
  74.5 0.0 copy-done.3
  74.5 0.0 copy-start.2
  74.5 0.0 copy-start.1
  74.5 0.8 %copy.16 = bf16[1024,256]{1,0:T(8,128)(2,1)} copy(bf16[1024,256]{1,0:T(8,128)(2,1)S(1)} %copy-done.3) | data formatting | bytes 1048576
  75.3 0.4 copy-done.2
  75.7 0.0 copy-start
  75.7 0.8 %copy.17 = bf16[1024,256]{1,0:T(8,128)(2,1)} copy(bf16[1024,256]{1,0:T(8,128)(2,1)S(1)} %copy-done.2) | data formatting | bytes 1048576
  76.5 0.0 copy-done.1
  76.5 0.8 %copy.18 = bf16[1024,256]{1,0:T(8,128)(2,1)} copy(bf16[1024,256]{1,0:T(8,128)(2,1)S(1)} %copy-done.1) | data formatting | bytes 1048576
  77.3 0.0 copy-done
  77.3 1.0 %copy.19 = f32[256,1024]{1,0:T(8,128)} copy(f32[256,1024]{1,0:T(8,128)S(1)} %copy-done) | data formatting | bytes 2097152
Async XLA Ops:
  72.5 1.9 %copy-start.3 = (bf16[1024,256]{1,0:T(8,128)(2,1)S(1)}, bf16[1024,256]{1,0:T(8,128)(2,1)}, u32[]{:S(2)}) copy-start(bf16[1024,256]{1,0:T(8,128)(2,1)} %get-tuple-element.11) | copy-start | bytes 1572868
  74.5 1.2 %copy-start.2 = (bf16[1024,256]{1,0:T(8,128)(2,1)S(1)}, bf16[1024,256]{1,0:T(8,128)(2,1)}, u32[]{:S(2)}) copy-start(bf16[1024,256]{1,0:T(8,128)(2,1)} %get-tuple-element.12) | copy-start | bytes 1572868
  74.5 2.0 %copy-start.1 = (bf16[1024,256]{1,0:T(8,128)(2,1)S(1)}, bf16[1024,256]{1,0:T(8,128)(2,1)}, u32[]{:S(2)}) copy-start(bf16[1024,256]{1,0:T(8,128)(2,1)} %get-tuple-element.13) | copy-start | bytes 1572868
  75.7 1.6 %copy-start = (f32[256,1024]{1,0:T(8,128)S(1)}, f32[256,1024]{1,0:T(8,128)}, u32[]{:S(2)}) copy-start(f32[256,1024]{1,0:T(8,128)} %get-tuple-element.14) | copy-start | bytes 3145732

commit v2 on v1

v2 whole, which is shorter than its diff:
```python
import functools

import jax
import jax.numpy as jnp
import numpy as np
from jax import lax
from jax.experimental import pallas as pl
from jax.experimental.pallas import tpu as pltpu
from jax.sharding import PartitionSpec as P

TILE = 128
DH = 128
STEP = 256
MESH = pl.DeviceIdType.MESH
F32 = jnp.float32
BF16 = jnp.bfloat16
NEG = -1e30
FAR = 3e38


def mm(a, b):
    return jnp.dot(a, b, preferred_element_type=F32)


def mm_t(a, b):
    return lax.dot_general(a, b, (((1,), (1,)), ((), ())), preferred_element_type=F32)


def kernel(
    plan,
    q_hbm, k_hbm, v_hbm, w_hbm, c_hbm,
    out_ref, dq_ref, dk_ref, dv_ref, wg_ref,
    q_ref, k_ref, v_ref, w_ref,
    ktile, vtile, kback, vback, ksend, vsend, vmid_f, kmid_b, vmid_b, vfar_b, one_b,
    cot, kt, vt, ktt, vtt,
    s_own, s_tile, e_own, e_tile, d_own, d_tile,
    acc, attn_t32, attn_t, attn, m_o, l_o, m_t, r_o, r_t, del_o, del_t,
    datt_t, datt_o, datt_s, datt_on, datt_sn, dqt,
    p_send, p_own, p_from,
    g_send, g_from, g_part, g_ysend, g_yfrom, g_y, g_zsend, g_zfrom, g_full,
    fwd_s, fwd_r, bwd_s, bwd_r, x_s, x_r, w_s, w_r, in_s,
):
    seq, heads_x, levels, ny, nz, ystride = plan
    rows, width = q_hbm.shape
    nh = width // DH
    nb = rows // STEP
    tail = rows - TILE
    b = lax.axis_index("seq")
    x = lax.axis_index("head")
    core = lax.rem(b, 2)
    yy = b // ystride
    zz = lax.rem(b, ystride) // 2
    right = lax.rem(x + 1, heads_x)
    left = lax.rem(x + heads_x - 1, heads_x)
    over = lax.rem(x + 2, heads_x)
    far = levels // 2
    factor = float(DH ** (-0.5) * np.log2(np.e))
    scale = DH ** (-0.5)

    def ahead(l):
        return (lax.rem(b + 2**l, seq), x)

    def behind(l):
        return (lax.rem(b + seq - 2**l, seq), x)

    sibling = (b + 1 - 2 * core, x)

    def ypeer(d):
        return lax.rem(yy + d, ny)

    def zpeer(d):
        return lax.rem(zz + d, nz)

    def yid(d):
        return (ypeer(d) * ystride + zz * 2 + core, x)

    def zid(d):
        return (yy * ystride + zpeer(d) * 2 + core, x)

    def from_z(dz):
        return yy * ystride + lax.rem(zz + dz + nz, nz) * 2 + core

    reach = 2**far
    mid_f = (from_z(-2), x)
    mid_b = (from_z(2), x)
    end_f = (lax.rem(from_z(2) + reach, seq), x)
    end_b = (lax.rem(from_z(-2) - reach + seq, seq), x)
    src_f, src_b = lax.rem(b + seq - reach, seq), lax.rem(b + reach, seq)
    pass_f = (src_f // ystride * ystride + lax.rem(lax.rem(src_f, ystride) // 2 + nz - 2, nz) * 2 + core, x)
    pass_b = (src_b // ystride * ystride + lax.rem(lax.rem(src_b, ystride) // 2 + 2, nz) * 2 + core, x)

    peers = [behind(0), ahead(0), behind(1), ahead(1), behind(far), ahead(far), pass_f, pass_b]
    peers += [yid(d) for d in range(1, ny)] + [zid(d) for d in range(1, nz)]
    peers += [(b, right), (b, left)]
    barrier = pltpu.get_barrier_semaphore()
    for peer in peers:
        pl.semaphore_signal(barrier, inc=1, device_id=peer, device_id_type=MESH)

    def remote(src, dst, sems, semr, idx, to):
        c = pltpu.make_async_remote_copy(
            src_ref=src, dst_ref=dst, send_sem=sems.at[idx], recv_sem=semr.at[idx],
            device_id=to, device_id_type=MESH,
        )
        c.start()
        return c

    def hs(h):
        return pl.ds(pl.multiple_of(h * DH, DH), DH)

    loads = [
        pltpu.make_async_copy(src, dst, in_s.at[n])
        for n, (src, dst) in enumerate(
            [(k_hbm, k_ref), (v_hbm, v_ref), (q_hbm, q_ref), (c_hbm, cot.at[x]), (w_hbm, w_ref)]
        )
    ]
    for c in loads:
        c.start()
    pl.semaphore_wait(barrier, len(peers))

    def rows_of(l):
        return pl.ds(l * TILE, TILE)

    sent = []
    ktc, vtc = {}, {}
    last = pl.ds(tail, TILE)

    def send_k(l):
        ktc[l] = remote(k_hbm.at[last], ktile.at[rows_of(l)], fwd_s, fwd_r, 2 * l, ahead(l))
        sent.append(ktc[l])

    def send_v(l):
        vtc[l] = remote(v_hbm.at[last], vtile.at[rows_of(l)], fwd_s, fwd_r, 2 * l + 1, ahead(l))
        sent.append(vtc[l])

    half = rows // 2
    lo, hi = pl.ds(0, half), pl.ds(half, half)
    mine = cot.at[x]
    send_k(1)
    send_v(1)
    v_mid = remote(v_hbm.at[last], vmid_f, fwd_s, fwd_r, 2 * levels, mid_f)
    to_right_lo = remote(c_hbm.at[lo], mine.at[lo], x_s, x_r, 0, (b, right))
    to_left_hi = remote(c_hbm.at[hi], mine.at[hi], x_s, x_r, 1, (b, left))
    send_k(far)
    send_k(0)
    send_v(0)
    for l in range(levels - 1, far, -1):
        send_k(l)
        send_v(l)
    to_right_hi = remote(c_hbm.at[hi], mine.at[hi], x_s, x_r, 2, (b, right))
    to_left_lo = remote(c_hbm.at[lo], mine.at[lo], x_s, x_r, 3, (b, left))
    sent += [v_mid, to_right_lo, to_left_hi, to_right_hi, to_left_lo]
    for c in loads:
        c.wait()
    kt[...] = k_ref[...].T
    vt[...] = v_ref[...].T

    def own_fwd(h, _):
        for i in range(nb):
            cols = pl.ds(i * STEP, STEP)
            qi = q_ref[cols, hs(h)]
            top = jnp.full((1, STEP), NEG, F32)
            for j in range(i + 1):
                s = mm_t(k_ref[pl.ds(j * STEP, STEP), hs(h)], qi)
                if j == i:
                    key = lax.broadcasted_iota(jnp.int32, (STEP, STEP), 0)
                    query = lax.broadcasted_iota(jnp.int32, (STEP, STEP), 1)
                    s = jnp.where(key <= query, s, NEG)
                s_own[pl.ds(j * STEP, STEP), :] = s
                top = jnp.maximum(top, jnp.max(s, axis=0, keepdims=True))
            m_o[h, :, cols] = top
            total = jnp.zeros((1, STEP), F32)
            part = jnp.zeros((DH, STEP), F32)
            for j in range(i + 1):
                e = jnp.exp2((s_own[pl.ds(j * STEP, STEP), :] - top) * factor)
                total = total + jnp.sum(e, axis=0, keepdims=True)
                e = e.astype(BF16)
                e_own[h, pl.ds(j * STEP, STEP), cols] = e
                part = part + mm(vt[hs(h), pl.ds(j * STEP, STEP)], e)
            l_o[h, :, cols] = total
            acc[hs(h), cols] = part
        return 0

    def forward_tiles():
        ktc[1].wait_recv()
        vtc[1].wait_recv()
        here, there = rows_of(1), rows_of(2)
        ktc[2] = remote(ktile.at[here], ktile.at[there], fwd_s, fwd_r, 4, ahead(1))
        vtc[2] = remote(vtile.at[here], vtile.at[there], fwd_s, fwd_r, 5, ahead(1))
        v_mid.wait_recv()
        vtc[far] = remote(vmid_f, vtile.at[rows_of(far)], fwd_s, fwd_r, 2 * far + 1, end_f)
        sent.extend([ktc[2], vtc[2], vtc[far]])

    own_fwd(0, 0)
    forward_tiles()
    for h in range(1, nh):
        own_fwd(h, 0)

    to_right_lo.wait_recv()
    pass_lo = remote(cot.at[left, lo], cot.at[left, lo], x_s, x_r, 4, (b, right))
    to_left_hi.wait_recv()
    pass_hi = remote(cot.at[right, hi], cot.at[right, hi], x_s, x_r, 5, (b, left))
    sent += [pass_lo, pass_hi]

    for h in range(nh):
        m_t[h] = jnp.full((1, rows), NEG, F32)
    valid = {l: b >= 2**l for l in range(levels)}
    arrive = list(range(levels - 1, far, -1)) + [1, 0, 2, far]
    for l in arrive:
        span = pl.ds(l * TILE, TILE)
        if l != 1:
            ktc[l].wait_recv()
            vtc[l].wait_recv()

        def tile_scores(h, _):
            for i in range(nb):
                cols = pl.ds(i * STEP, STEP)
                s = mm_t(ktile[span, hs(h)], q_ref[cols, hs(h)])
                s_tile[h, span, cols] = s
                top = jnp.max(s, axis=0, keepdims=True)
                m_t[h, :, cols] = jnp.maximum(m_t[h, :, cols], jnp.where(valid[l], top, NEG))
            return 0

        lax.fori_loop(0, nh, tile_scores, 0)
        ktt[:, span] = ktile[span, :].T
        vtt[:, span] = vtile[span, :].T

    def tile_fwd(h, _):
        for i in range(nb):
            cols = pl.ds(i * STEP, STEP)
            top = m_t[h, :, cols]
            total = jnp.zeros((1, STEP), F32)
            part = jnp.zeros((DH, STEP), F32)
            for l in range(levels):
                span = pl.ds(l * TILE, TILE)
                shift = jnp.where(valid[l], top, FAR)
                e = jnp.exp2((s_tile[h, span, cols] - shift) * factor)
                total = total + jnp.sum(e, axis=0, keepdims=True)
                e_tile[h, span, cols] = e.astype(BF16)
            part = mm(vtt[hs(h), :], e_tile[h, :, cols])
            mo = m_o[h, :, cols]
            m = jnp.maximum(mo, top)
            fo = jnp.exp2((mo - m) * factor)
            ft = jnp.exp2((top - m) * factor)
            inv = 1.0 / (fo * l_o[h, :, cols] + ft * total)
            fo = fo * inv
            ft = ft * inv
            r_o[h, :, cols] = fo
            r_t[h, :, cols] = ft
            at = acc[hs(h), cols] * fo + part * ft
            attn_t32[hs(h), cols] = at
            attn_t[hs(h), cols] = at.astype(BF16)
            attn[cols, hs(h)] = at.T.astype(BF16)
        return 0

    lax.fori_loop(0, nh, tile_fwd, 0)

    gh = width // 2
    gy = gh // ny
    gz = heads_x * width // nz
    at_rows = pl.ds(pl.multiple_of(core * gh + yy * gy, gy), gy)
    copies = {}

    def wcols(at):
        return pl.ds(pl.multiple_of(at * width, width), width)

    def yrows(at):
        return pl.ds(pl.multiple_of(at * gy, gy), gy)

    def zcols(at):
        return pl.ds(pl.multiple_of(at * gz, gz), gz)

    def half_rows(at):
        return pl.ds(pl.multiple_of(at * gh, gh), gh)

    def keep(name, *made):
        copies[name] = list(made)
        sent.extend(made)

    def arrived(name):
        for c in copies[name]:
            c.wait_recv()

    def out_over():
        p_send[0] = mm(attn[...], w_ref[:, wcols(over)]).astype(BF16)
        keep("o_lo", remote(p_send.at[0, lo], p_from.at[0, lo], x_s, x_r, 6, (b, right)))
        keep("o_hi", remote(p_send.at[0, hi], p_from.at[1, hi], x_s, x_r, 7, (b, left)))

    def out_next():
        p_send[1] = mm(attn[...], w_ref[:, wcols(right)]).astype(BF16)
        c = remote(p_send.at[1, hi], p_from.at[2, hi], x_s, x_r, 8, (b, right))
        p_send[2] = mm(attn[...], w_ref[:, wcols(left)]).astype(BF16)
        keep("near", c, remote(p_send.at[2, lo], p_from.at[3, lo], x_s, x_r, 9, (b, left)))

    def out_own():
        p_own[...] = mm(attn[...], w_ref[:, wcols(x)])

    def out_pass():
        arrived("o_lo")
        p_send[1, lo, :] = (p_send[1, lo, :].astype(F32) + p_from[0, lo, :].astype(F32)).astype(BF16)
        c = remote(p_send.at[1, lo], p_from.at[2, lo], x_s, x_r, 10, (b, right))
        arrived("o_hi")
        p_send[2, hi, :] = (p_send[2, hi, :].astype(F32) + p_from[1, hi, :].astype(F32)).astype(BF16)
        keep("passed", c, remote(p_send.at[2, hi], p_from.at[3, hi], x_s, x_r, 11, (b, left)))

    def out_end():
        arrived("near")
        arrived("passed")
        out_ref[...] = (p_own[...] + p_from[2].astype(F32) + p_from[3].astype(F32)).astype(BF16)

    def cot_all():
        to_right_hi.wait_recv()
        to_left_lo.wait_recv()
        pass_lo.wait_recv()
        pass_hi.wait_recv()

    def wg_other():
        for j in range(heads_x):
            g_send[:, pl.ds(j * width, width)] = mm(attn_t[half_rows(1 - core), :], cot[j]).astype(BF16)
        keep("core", remote(g_send, g_from, w_s, w_r, 0, sibling))

    def wg_mine():
        for j in range(heads_x):
            g_part[:, pl.ds(j * width, width)] = mm(attn_t[half_rows(core), :], cot[j])

    def wg_y():
        arrived("core")
        g_part[...] = g_part[...] + g_from[...].astype(F32)
        g_ysend[...] = g_part[...].astype(BF16)
        keep("ysum", *[
            remote(g_ysend.at[yrows(ypeer(d))], g_yfrom.at[d], w_s, w_r, d, yid(d)) for d in range(1, ny)
        ])

    def wg_z():
        arrived("ysum")
        total = g_part[yrows(yy), :]
        for d in range(1, ny):
            total = total + g_yfrom[d].astype(F32)
        g_y[...] = total
        g_zsend[...] = total.astype(BF16)
        keep("zsum", *[
            remote(g_zsend.at[:, zcols(zpeer(d))], g_zfrom.at[d], w_s, w_r, ny + d, zid(d))
            for d in range(1, nz)
        ])

    def wg_z_back():
        arrived("zsum")
        piece = g_y[:, zcols(zz)]
        for d in range(1, nz):
            piece = piece + g_zfrom[d].astype(F32)
        own = g_full.at[at_rows, zcols(zz)]
        g_full[at_rows, zcols(zz)] = piece.astype(BF16)
        keep("zall", *[remote(own, own, w_s, w_r, ny + nz + d, zid(d)) for d in range(1, nz)])

    def wg_y_back():
        arrived("zall")
        own = g_full.at[at_rows]
        made = [remote(own, own, w_s, w_r, ny + 2 * nz + d, yid(d)) for d in range(1, ny)]
        made.append(remote(own, own, w_s, w_r, 2 * ny + 2 * nz, sibling))
        keep("yall", *made[:-1])
        keep("last", made[-1])

    def wg_core_back():
        made = []
        for d in range(1, ny):
            copies["yall"][d - 1].wait_recv()
            rows_d = pl.ds(pl.multiple_of(core * gh + lax.rem(yy + ny - d, ny) * gy, gy), gy)
            got = g_full.at[rows_d]
            made.append(remote(got, got, w_s, w_r, 2 * ny + 2 * nz + d, sibling))
        keep("lasts", *made)

    def wg_end():
        arrived("last")
        arrived("lasts")
        wg_ref[...] = g_full[...].astype(F32)

    def dattn():
        for i in range(nb):
            cols = pl.ds(i * STEP, STEP)
            g = jnp.zeros((width, STEP), F32)
            for j in range(heads_x):
                g = g + mm_t(w_ref[:, pl.ds(j * width, width)], cot[j, cols, :])
            datt_t[:, cols] = g.astype(BF16)

    def spread_head(h, _):
        for i in range(nb):
            cols = pl.ds(i * STEP, STEP)
            g = datt_t[hs(h), cols].astype(F32)
            at = attn_t32[hs(h), cols]
            go = (g * r_o[h, :, cols]).astype(BF16)
            gt = (g * r_t[h, :, cols]).astype(BF16)
            datt_o[hs(h), cols] = go
            datt_s[hs(h), cols] = gt
            go = go.astype(F32)
            gt = gt.astype(F32)
            del_o[h, :, cols] = jnp.sum(go * at, axis=0, keepdims=True)
            del_t[h, :, cols] = jnp.sum(gt * at, axis=0, keepdims=True)
            datt_on[cols, hs(h)] = go.T.astype(BF16)
            datt_sn[cols, hs(h)] = gt.T.astype(BF16)
        return 0

    def spread():
        lax.fori_loop(0, nh, spread_head, 0)

    kbc, vbc = {}, {}

    def tile_bwd_for(l):
        span = rows_of(l)

        def tile_bwd(h, _):
            for i in range(nb):
                cols = pl.ds(i * STEP, STEP)
                dp = mm(vtile[span, hs(h)], datt_s[hs(h), cols])
                d = e_tile[h, span, cols].astype(F32) * (dp - del_t[h, :, cols])
                d_tile[h, span, cols] = d.astype(BF16)
            dk = mm(d_tile[h, span, :], q_ref[:, hs(h)]) * scale
            dv = mm(e_tile[h, span, :], datt_sn[:, hs(h)])
            if l == 1:
                one_b[0, :, hs(h)] = dk
                one_b[1, :, hs(h)] = dv
            else:
                ksend[span, hs(h)] = dk.astype(BF16)
                vsend[span, hs(h)] = dv.astype(BF16)
            return 0

        lax.fori_loop(0, nh, tile_bwd, 0)

    def back_k(l, to, dst):
        kbc[l] = remote(ksend.at[rows_of(l)], dst, bwd_s, bwd_r, 2 * l, to)
        sent.append(kbc[l])

    def back_v(l, to, dst):
        vbc[l] = remote(vsend.at[rows_of(l)], dst, bwd_s, bwd_r, 2 * l + 1, to)
        sent.append(vbc[l])

    def tile_two():
        tile_bwd_for(2)
        back_k(2, behind(1), kmid_b)
        back_v(2, behind(1), vmid_b)

    def tile_far():
        tile_bwd_for(far)
        back_v(far, mid_b, vfar_b)
        back_k(far, behind(far), kback.at[rows_of(far)])

    def tile_one():
        tile_bwd_for(1)

    def tile_one_send():
        kbc[2].wait_recv()
        vbc[2].wait_recv()
        ksend[rows_of(1), :] = (one_b[0] + kmid_b[...].astype(F32)).astype(BF16)
        vsend[rows_of(1), :] = (one_b[1] + vmid_b[...].astype(F32)).astype(BF16)
        back_k(1, behind(1), kback.at[rows_of(1)])
        back_v(1, behind(1), vback.at[rows_of(1)])

    def tile_far_pass():
        vbc[far].wait_recv()
        vbc[far] = remote(vfar_b, vback.at[rows_of(far)], bwd_s, bwd_r, 2 * levels, end_b)
        sent.append(vbc[far])

    def tile_direct(l):
        tile_bwd_for(l)
        back_k(l, behind(l), kback.at[rows_of(l)])
        back_v(l, behind(l), vback.at[rows_of(l)])

    def tile_zero():
        tile_direct(0)

    def tile_y():
        for l in range(levels - 1, far, -1):
            tile_direct(l)

    def tile_end():
        dk = dqt[0]
        dv = dqt[1]
        for l in [0, 1, far] + list(range(far + 1, levels)):
            span = rows_of(l)
            kbc[l].wait_recv()
            vbc[l].wait_recv()
            dk = dk + kback[span, :].astype(F32)
            dv = dv + vback[span, :].astype(F32)
        dk_ref[last, :] = dk.astype(BF16)
        dv_ref[last, :] = dv.astype(BF16)

    def own_keys(h, j):
        span = pl.ds(j * STEP, STEP)
        for i in range(j, nb):
            cols = pl.ds(i * STEP, STEP)
            dp = mm(v_ref[span, hs(h)], datt_o[hs(h), cols])
            d = e_own[h, span, cols].astype(F32) * (dp - del_o[h, :, cols])
            d_own[h, span, cols] = d.astype(BF16)
        rest = pl.ds(j * STEP, rows - j * STEP)
        dk = mm(d_own[h, span, rest], q_ref[rest, hs(h)]) * scale
        dv = mm(e_own[h, span, rest], datt_on[rest, hs(h)])
        dk_ref[span, hs(h)] = dk.astype(BF16)
        dv_ref[span, hs(h)] = dv.astype(BF16)
        if j == nb - 1:
            dqt[0, :, hs(h)] = dk[STEP - TILE :]
            dqt[1, :, hs(h)] = dv[STEP - TILE :]

    def own_a():
        for h in range(nh):
            own_keys(h, 0)

    def own_b():
        for h in range(nh):
            for j in range(1, nb):
                own_keys(h, j)

    def own_q():
        for h in range(nh):
            for i in range(nb):
                cols = pl.ds(i * STEP, STEP)
                upto = pl.ds(0, (i + 1) * STEP)
                g = mm(kt[hs(h), upto], d_own[h, upto, cols])
                g = g + mm(ktt[hs(h), :], d_tile[h, :, cols])
                dq_ref[cols, hs(h)] = (g * scale).T.astype(BF16)

    for step in (
cot_all, wg_other, wg_mine, out_over, wg_y, out_next, dattn, spread, own_a, wg_z, tile_two, own_b, wg_z_back, tile_far, tile_zero, tile_one, tile_one_send, wg_y_back, tile_far_pass, tile_y, out_pass, out_own, wg_core_back, own_q, tile_end, wg_end, out_end,
    ):
        step()

    for c in sent:
        c.wait_send()


def local(plan, queries, keys, values, out_weight, cotangent):
    seq, heads_x, levels, ny, nz, _ = plan
    rows, width = queries.shape
    nh = width // DH
    far = levels * TILE
    wide = heads_x * width
    gh = width // 2
    gy = gh // ny
    gz = wide // nz
    dma = pltpu.SemaphoreType.DMA
    like = [(rows, width)] * 4
    return pl.pallas_call(
        functools.partial(kernel, plan),
        out_shape=[pltpu.VMEM(s, BF16) for s in like] + [pltpu.VMEM((width, wide), F32)],
        in_specs=[pl.BlockSpec(memory_space=pl.ANY)] * 5,
        out_specs=[pl.BlockSpec(memory_space=pltpu.VMEM)] * 5,
        scratch_shapes=[
            pltpu.VMEM((rows, width), BF16), pltpu.VMEM((rows, width), BF16),
            pltpu.VMEM((rows, width), BF16), pltpu.VMEM((width, wide), BF16),
            pltpu.VMEM((far, width), BF16), pltpu.VMEM((far, width), BF16),
            pltpu.VMEM((far, width), BF16), pltpu.VMEM((far, width), BF16),
            pltpu.VMEM((far, width), BF16), pltpu.VMEM((far, width), BF16),
            pltpu.VMEM((TILE, width), BF16), pltpu.VMEM((TILE, width), BF16),
            pltpu.VMEM((TILE, width), BF16), pltpu.VMEM((TILE, width), BF16),
            pltpu.VMEM((2, TILE, width), F32),
            pltpu.VMEM((heads_x, rows, width), BF16),
            pltpu.VMEM((width, rows), BF16), pltpu.VMEM((width, rows), BF16),
            pltpu.VMEM((width, far), BF16), pltpu.VMEM((width, far), BF16),
            pltpu.VMEM((rows, STEP), F32), pltpu.VMEM((nh, far, rows), F32),
            pltpu.VMEM((nh, rows, rows), BF16), pltpu.VMEM((nh, far, rows), BF16),
            pltpu.VMEM((nh, rows, rows), BF16), pltpu.VMEM((nh, far, rows), BF16),
            pltpu.VMEM((width, rows), F32), pltpu.VMEM((width, rows), F32),
            pltpu.VMEM((width, rows), BF16), pltpu.VMEM((rows, width), BF16),
        ]
        + [pltpu.VMEM((nh, 1, rows), F32)] * 7
        + [
            pltpu.VMEM((width, rows), BF16), pltpu.VMEM((width, rows), BF16),
            pltpu.VMEM((width, rows), BF16), pltpu.VMEM((rows, width), BF16),
            pltpu.VMEM((rows, width), BF16), pltpu.VMEM((2, TILE, width), F32),
            pltpu.VMEM((3, rows, width), BF16), pltpu.VMEM((rows, width), F32),
            pltpu.VMEM((4, rows, width), BF16),
            pltpu.VMEM((gh, wide), BF16), pltpu.VMEM((gh, wide), BF16),
            pltpu.VMEM((gh, wide), F32), pltpu.VMEM((gh, wide), BF16),
            pltpu.VMEM((ny, gy, wide), BF16), pltpu.VMEM((gy, wide), F32),
            pltpu.VMEM((gy, wide), BF16), pltpu.VMEM((nz, gy, gz), BF16),
            pltpu.VMEM((width, wide), BF16),
            dma((2 * levels + 1,)), dma((2 * levels + 1,)), dma((2 * levels + 1,)), dma((2 * levels + 1,)),
            dma((12,)), dma((12,)),
            dma((3 * ny + 2 * nz,)), dma((3 * ny + 2 * nz,)), dma((5,)),
        ],
        compiler_params=pltpu.CompilerParams(
            collective_id=0, has_side_effects=True, vmem_limit_bytes=52 * 1024 * 1024
        ),
        name="layer",
    )(queries, keys, values, out_weight, cotangent)


def solution(mesh):
    seq = mesh.shape["seq"]
    heads_x = mesh.shape["head"]
    levels = seq.bit_length() - 1
    ny = 4 if seq >= 16 else 2
    ystride = seq // ny
    plan = (seq, heads_x, levels, ny, ystride // 2, ystride)
    return jax.shard_map(
        functools.partial(local, plan),
        mesh=mesh,
        in_specs=(
            P("seq", "head"), P("seq", "head"), P("seq", "head"), P("head", None), P("seq", "head"),
        ),
        out_specs=(
            P("seq", "head"), P("seq", "head"), P("seq", "head"), P("seq", "head"), P("head", None),
        ),
        check_vma=False,
    )
```

time: 78.4 us -> 65.1 us (0.83); the launches traced: 78.3 us -> 63.9 us
  Pallas kernels: 71.9 us -> 59.1 us
  local copies, waits for them, and re-layouts: 5.72 us -> 4.14 us
    pallas_call x1, Pallas kernels: 71.9 us -> 59.1 us  [local(): pl.pallas_call(functools.partial(kernel, plan), out_shape=[pltpu.VMEM(s,...]
    unnamed x13 -> x5, local copies, waits for them, and re-layouts: 5.72 us -> 4.14 us
where the time goes in v2:
time: 65.1 us; the launch traced here: 63.9 us
  Pallas kernels  59.1 us (91%)
  local copies, waits for them, and re-layouts  4.14 us (6%)
    pallas_call x1, Pallas kernels, local(): pl.pallas_call(functools.partial(kernel, plan), out_shape=[pltpu.VMEM(s,...  59.1 us
    unnamed x5, local copies, waits for them, and re-layouts  4.14 us

profile of v2, /device:TPU:1, one launch (start us, length us, event | category | flops | bytes accessed | tf_op | source)
XLA Modules:
  0.0 63.9 jit_solution(6643494447773053487)
XLA Ops:
  0.6 59.1 %layer.1 = (bf16[1024,256]{1,0:T(8,128)(2,1)S(1)}, bf16[1024,256]{1,0:T(8,128)(2,1)S(1)}, bf16[1024,256]{1,0:T(8,128)(2,1)S(1)}, bf16[1024,256]{1,0:T(8,128)(2,1)S(1)}, f32[256,1024]{1,0:T(8,128)S(1)}) custom-call(bf16[1024,256]{1,0:T(8,128)(2,1)} %q_hbm.1, bf16[1024,256]{1,0:T(8,128)(2,1)} %k_hbm.1, bf16[1024,256]{1,0:T(8,128)(2,1)} %v_hbm.1, ...), custom_call_target="tpu_custom_call" | custom-call | tf_op jit(solution)/shard_map/layer/pallas_call | solution.py:539
  59.7 0.8 %copy.15 = bf16[1024,256]{1,0:T(8,128)(2,1)} copy(bf16[1024,256]{1,0:T(8,128)(2,1)S(1)} %get-tuple-element.5) | data formatting | bytes 1048576
  60.5 0.8 %copy.16 = bf16[1024,256]{1,0:T(8,128)(2,1)} copy(bf16[1024,256]{1,0:T(8,128)(2,1)S(1)} %get-tuple-element.6) | data formatting | bytes 1048576
  61.3 0.8 %copy.17 = bf16[1024,256]{1,0:T(8,128)(2,1)} copy(bf16[1024,256]{1,0:T(8,128)(2,1)S(1)} %get-tuple-element.7) | data formatting | bytes 1048576
  62.1 0.8 %copy.18 = bf16[1024,256]{1,0:T(8,128)(2,1)} copy(bf16[1024,256]{1,0:T(8,128)(2,1)S(1)} %get-tuple-element.8) | data formatting | bytes 1048576
  62.9 1.0 %copy.19 = f32[256,1024]{1,0:T(8,128)} copy(f32[256,1024]{1,0:T(8,128)S(1)} %get-tuple-element.9) | data formatting | bytes 2097152

commit v3 on v2

--- a/solution.py
+++ b/solution.py
@@ -204,20 +204,23 @@
     for h in range(nh):
         m_t[h] = jnp.full((1, rows), NEG, F32)
     valid = {l: b >= 2**l for l in range(levels)}
-    arrive = list(range(levels - 1, far, -1)) + [1, 0, 2, far]
-    for l in arrive:
-        span = pl.ds(l * TILE, TILE)
-        if l != 1:
-            ktc[l].wait_recv()
-            vtc[l].wait_recv()
+    for pair in (levels - 2, 0, far - 1):
+        span = pl.ds(pair * TILE, 2 * TILE)
+        for l in (pair, pair + 1):
+            if l != 1:
+                ktc[l].wait_recv()
+                vtc[l].wait_recv()
 
         def tile_scores(h, _):
             for i in range(nb):
                 cols = pl.ds(i * STEP, STEP)
                 s = mm_t(ktile[span, hs(h)], q_ref[cols, hs(h)])
                 s_tile[h, span, cols] = s
-                top = jnp.max(s, axis=0, keepdims=True)
-                m_t[h, :, cols] = jnp.maximum(m_t[h, :, cols], jnp.where(valid[l], top, NEG))
+                top = jnp.max(s[:TILE], axis=0, keepdims=True)
+                second = jnp.max(s[TILE:], axis=0, keepdims=True)
+                top = jnp.where(valid[pair], top, NEG)
+                second = jnp.where(valid[pair + 1], second, NEG)
+                m_t[h, :, cols] = jnp.maximum(m_t[h, :, cols], jnp.maximum(top, second))
             return 0
 
         lax.fori_loop(0, nh, tile_scores, 0)
@@ -403,8 +406,8 @@
 
     kbc, vbc = {}, {}
 
-    def tile_bwd_for(l):
-        span = rows_of(l)
+    def tile_bwd_for(pair):
+        span = pl.ds(pair * TILE, 2 * TILE)
 
         def tile_bwd(h, _):
             for i in range(nb):
@@ -414,12 +417,11 @@
                 d_tile[h, span, cols] = d.astype(BF16)
             dk = mm(d_tile[h, span, :], q_ref[:, hs(h)]) * scale
             dv = mm(e_tile[h, span, :], datt_sn[:, hs(h)])
-            if l == 1:
-                one_b[0, :, hs(h)] = dk
-                one_b[1, :, hs(h)] = dv
-            else:
-                ksend[span, hs(h)] = dk.astype(BF16)
-                vsend[span, hs(h)] = dv.astype(BF16)
+            if pair == 0:
+                one_b[0, :, hs(h)] = dk[TILE:]
+                one_b[1, :, hs(h)] = dv[TILE:]
+            ksend[span, hs(h)] = dk.astype(BF16)
+            vsend[span, hs(h)] = dv.astype(BF16)
             return 0
 
         lax.fori_loop(0, nh, tile_bwd, 0)
@@ -432,18 +434,16 @@
         vbc[l] = remote(vsend.at[rows_of(l)], dst, bwd_s, bwd_r, 2 * l + 1, to)
         sent.append(vbc[l])
 
-    def tile_two():
-        tile_bwd_for(2)
+    def tile_z():
+        tile_bwd_for(far - 1)
         back_k(2, behind(1), kmid_b)
         back_v(2, behind(1), vmid_b)
-
-    def tile_far():
-        tile_bwd_for(far)
         back_v(far, mid_b, vfar_b)
         back_k(far, behind(far), kback.at[rows_of(far)])
 
-    def tile_one():
-        tile_bwd_for(1)
+    def tile_near():
+        tile_bwd_for(0)
+        tile_direct(0)
 
     def tile_one_send():
         kbc[2].wait_recv()
@@ -459,14 +459,11 @@
         sent.append(vbc[far])
 
     def tile_direct(l):
-        tile_bwd_for(l)
         back_k(l, behind(l), kback.at[rows_of(l)])
         back_v(l, behind(l), vback.at[rows_of(l)])
 
-    def tile_zero():
-        tile_direct(0)
-
     def tile_y():
+        tile_bwd_for(levels - 2)
         for l in range(levels - 1, far, -1):
             tile_direct(l)
 
@@ -517,12 +514,21 @@
                 dq_ref[cols, hs(h)] = (g * scale).T.astype(BF16)
 
     for step in (
-cot_all, wg_other, wg_mine, out_over, wg_y, out_next, dattn, spread, own_a, wg_z, tile_two, own_b, wg_z_back, tile_far, tile_zero, tile_one, tile_one_send, wg_y_back, tile_far_pass, tile_y, out_pass, out_own, wg_core_back, own_q, tile_end, wg_end, out_end,
+cot_all, wg_other, wg_mine, out_over, wg_y, out_next, dattn, spread, own_a, wg_z, tile_z, tile_near, wg_z_back, tile_one_send, wg_y_back, tile_far_pass, tile_y, own_b, out_pass, out_own, wg_core_back, own_q, wg_end, tile_end, out_end,
     ):
         step()
 
     for c in sent:
         c.wait_send()
+
+
+def store(*refs):
+    n = len(refs) // 2
+    made = [pltpu.make_async_copy(refs[i], refs[n + i], refs[-1].at[i]) for i in range(n)]
+    for c in made:
+        c.start()
+    for c in made:
+        c.wait()
 
 
 def local(plan, queries, keys, values, out_weight, cotangent):
@@ -536,7 +542,8 @@
     gz = wide // nz
     dma = pltpu.SemaphoreType.DMA
     like = [(rows, width)] * 4
-    return pl.pallas_call(
+    shapes = [jax.ShapeDtypeStruct(s, BF16) for s in like] + [jax.ShapeDtypeStruct((width, wide), F32)]
+    made = pl.pallas_call(
         functools.partial(kernel, plan),
         out_shape=[pltpu.VMEM(s, BF16) for s in like] + [pltpu.VMEM((width, wide), F32)],
         in_specs=[pl.BlockSpec(memory_space=pl.ANY)] * 5,
@@ -580,6 +587,14 @@
         ),
         name="layer",
     )(queries, keys, values, out_weight, cotangent)
+    return pl.pallas_call(
+        store,
+        out_shape=shapes,
+        in_specs=[pl.BlockSpec(memory_space=pltpu.VMEM)] * 5,
+        out_specs=[pl.BlockSpec(memory_space=pl.ANY)] * 5,
+        scratch_shapes=[dma((5,))],
+        name="store",
+    )(*[pltpu.with_memory_space_constraint(a, pltpu.VMEM) for a in made])
 
 
 def solution(mesh):

time: 65.1 us -> 62.7 us (0.963); the launches traced: 63.9 us -> 62.5 us
  local copies, waits for them, and re-layouts: 4.14 us -> 0 us
  Pallas kernels: 59.1 us -> 61.7 us
    unnamed x5 -> x0, local copies, waits for them, and re-layouts: 4.14 us -> none
    pallas_call x0 -> x1, Pallas kernels: none -> 1.71 us  [local(): pl.pallas_call(store, out_shape=shapes, in_specs=[pl.BlockSpec(memory_spa...]
    pallas_call x1, Pallas kernels: 59.1 us -> 60 us  [local(): pl.pallas_call(functools.partial(kernel, plan), out_shape=[pltpu.VMEM(s,...]
where the time goes in v3:
time: 62.7 us; the launch traced here: 62.5 us
  Pallas kernels  61.7 us (98%)
  between operations  0.8 us (1%)
    pallas_call x1, Pallas kernels, local(): pl.pallas_call(functools.partial(kernel, plan), out_shape=[pltpu.VMEM(s,...  60 us
    pallas_call x1, Pallas kernels, local(): pl.pallas_call(store, out_shape=shapes, in_specs=[pl.BlockSpec(memory_spa...  1.71 us

profile of v3, /device:TPU:1, one launch (start us, length us, event | category | flops | bytes accessed | tf_op | source)
XLA Modules:
  0.0 62.5 jit_solution(3761577838832507385)
XLA Ops:
  0.6 60.0 %layer.1 = (bf16[1024,256]{1,0:T(8,128)(2,1)S(1)}, bf16[1024,256]{1,0:T(8,128)(2,1)S(1)}, bf16[1024,256]{1,0:T(8,128)(2,1)S(1)}, bf16[1024,256]{1,0:T(8,128)(2,1)S(1)}, f32[256,1024]{1,0:T(8,128)S(1)}) custom-call(bf16[1024,256]{1,0:T(8,128)(2,1)} %q_hbm.1, bf16[1024,256]{1,0:T(8,128)(2,1)} %k_hbm.1, bf16[1024,256]{1,0:T(8,128)(2,1)} %v_hbm.1, ...), custom_call_target="tpu_custom_call" | custom-call | tf_op jit(solution)/shard_map/layer/pallas_call | solution.py:546
  60.7 1.7 %store.1 = (bf16[1024,256]{1,0:T(8,128)(2,1)}, bf16[1024,256]{1,0:T(8,128)(2,1)}, bf16[1024,256]{1,0:T(8,128)(2,1)}, bf16[1024,256]{1,0:T(8,128)(2,1)}, f32[256,1024]{1,0:T(8,128)}) custom-call(bf16[1024,256]{1,0:T(8,128)(2,1)S(1)} %get-tuple-element.10.refs_0_, bf16[1024,256]{1,0:T(8,128)(2,1)S(1)} %get-tuple-element.11.refs_1_, ...), custom_call_target="tpu_custom_call" | custom-call | tf_op jit(solution)/shard_map/store/pallas_call | solution.py:590

commit v4 on v3

--- a/solution.py
+++ b/solution.py
@@ -514,7 +514,7 @@
                 dq_ref[cols, hs(h)] = (g * scale).T.astype(BF16)
 
     for step in (
-cot_all, wg_other, wg_mine, out_over, wg_y, out_next, dattn, spread, own_a, wg_z, tile_z, tile_near, wg_z_back, tile_one_send, wg_y_back, tile_far_pass, tile_y, own_b, out_pass, out_own, wg_core_back, own_q, wg_end, tile_end, out_end,
+cot_all, wg_other, wg_mine, out_over, wg_y, out_next, dattn, spread, own_a, wg_z, tile_z, tile_near, wg_z_back, tile_one_send, wg_y_back, tile_far_pass, tile_y, out_pass, own_b, out_own, wg_core_back, own_q, wg_end, tile_end, out_end,
     ):
         step()
 

time: 62.7 us -> 62.7 us (level)
  no operation moved by 1% of the time
where the time goes in v4:
time: 62.7 us; the launch traced here: 62.5 us
  Pallas kernels  61.7 us (98%)
  between operations  0.8 us (1%)
    pallas_call x1, Pallas kernels, local(): pl.pallas_call(functools.partial(kernel, plan), out_shape=[pltpu.VMEM(s,...  60 us
    pallas_call x1, Pallas kernels, local(): pl.pallas_call(store, out_shape=shapes, in_specs=[pl.BlockSpec(memory_spa...  1.71 us

profile of v4, /device:TPU:1, one launch (start us, length us, event | category | flops | bytes accessed | tf_op | source)
XLA Modules:
  0.0 62.5 jit_solution(18111263003042292171)
XLA Ops:
  0.6 60.0 %layer.1 = (bf16[1024,256]{1,0:T(8,128)(2,1)S(1)}, bf16[1024,256]{1,0:T(8,128)(2,1)S(1)}, bf16[1024,256]{1,0:T(8,128)(2,1)S(1)}, bf16[1024,256]{1,0:T(8,128)(2,1)S(1)}, f32[256,1024]{1,0:T(8,128)S(1)}) custom-call(bf16[1024,256]{1,0:T(8,128)(2,1)} %q_hbm.1, bf16[1024,256]{1,0:T(8,128)(2,1)} %k_hbm.1, bf16[1024,256]{1,0:T(8,128)(2,1)} %v_hbm.1, ...), custom_call_target="tpu_custom_call" | custom-call | tf_op jit(solution)/shard_map/layer/pallas_call | solution.py:546
  60.7 1.7 %store.1 = (bf16[1024,256]{1,0:T(8,128)(2,1)}, bf16[1024,256]{1,0:T(8,128)(2,1)}, bf16[1024,256]{1,0:T(8,128)(2,1)}, bf16[1024,256]{1,0:T(8,128)(2,1)}, f32[256,1024]{1,0:T(8,128)}) custom-call(bf16[1024,256]{1,0:T(8,128)(2,1)S(1)} %get-tuple-element.10.refs_0_, bf16[1024,256]{1,0:T(8,128)(2,1)S(1)} %get-tuple-element.11.refs_1_, ...), custom_call_target="tpu_custom_call" | custom-call | tf_op jit(solution)/shard_map/store/pallas_call | solution.py:590
